TPU v7x, 512 devices: a whole 4x4x16 slice. The times are simulated.
512 devices in a mesh: wa: 128 (over z, x, y_hi), gx: 4 (over y_lo, core).
Axes of the slice: x: 4, y: 4 (y_hi: 2, y_lo: 2; y = y_hi * 2 + y_lo), z: 16, core: 2. Of those that a mesh axis runs over, the one named last changes fastest.
Arguments:
- field_a: float32 [2, 4, 768, 3840], P(None, 'gx', 'wa'), may hold values from -6 to 6
- field_b: float32 [2, 4, 768, 3840], P(None, 'gx', 'wa'), may hold values from -6 to 6
- keep_mask: int32 [3840], replicated, may hold values 0 or 1
- block_inv: float32 [6, 128, 128], replicated
- lower_mult: float32 [5, 128, 128], replicated, may hold values from -0.15 to 0.15
Outputs:
- new_a: float32 [2, 4, 768, 3840], P(None, 'gx', 'wa')
- new_b: float32 [2, 4, 768, 3840], P(None, 'gx', 'wa')
All inputs are finite; a program needn't handle non-finite values.
Results may differ from a plain program's by a relative error of at most 0.0001.
Values sent between devices are 32-bit elements; how exact they have to be, the bound alone decides.
No kernel may reach another device: no remote copies, remote signals or barrier semaphores. Data moves between devices by JAX's collectives and lax.ppermute only.
A program may use at most 64 MiB of HBM per device.

v0:
```python
import math

import jax
import jax.numpy as jnp
import ml_dtypes
import numpy as np
from jax import lax
from jax.experimental import pallas as pl
from jax.experimental.pallas import tpu as pltpu
from jax.sharding import PartitionSpec as P

NL_COEFF = 0.25
BF16 = ml_dtypes.bfloat16

LANES = 128
OUTER = 45
KEPT = 30
ROWS = 6
SLOT = 48
PARTS = 2 * ROWS * KEPT


def split_np(table):
    high = table.astype(np.float32).astype(BF16)
    low = (table - high.astype(np.float64)).astype(np.float32).astype(BF16)
    return high, low


def build_tables():
    modes = KEPT * LANES
    length = OUTER * LANES
    half = KEPT // 2
    kept = np.array([j if j < half else j + OUTER - KEPT for j in range(KEPT)])
    n1 = np.arange(OUTER)
    lane = np.arange(LANES)
    short = 2.0 * np.pi * ((n1[:, None] * kept[None, :]) % OUTER) / OUTER
    to_grid = np.zeros((2 * SLOT, 64))
    scale = 1.0 / math.sqrt(modes)
    to_grid[:OUTER, 0:KEPT] = np.cos(short) * scale
    to_grid[:OUTER, 34:64] = -np.sin(short) * scale
    to_grid[SLOT : SLOT + OUTER, 0:KEPT] = np.sin(short) * scale
    to_grid[SLOT : SLOT + OUTER, 34:64] = np.cos(short) * scale
    to_modes = np.zeros((64, 2 * SLOT))
    scale = NL_COEFF / math.sqrt(length)
    to_modes[0:KEPT, :OUTER] = np.cos(short).T * scale
    to_modes[0:KEPT, SLOT : SLOT + OUTER] = -np.sin(short).T * scale
    to_modes[34:64, :OUTER] = -np.sin(short).T * scale
    to_modes[34:64, SLOT : SLOT + OUTER] = -np.cos(short).T * scale
    twist = 2.0 * np.pi * (n1[:, None] * lane[None, :]) / length
    twist_re = np.zeros((SLOT, LANES), np.float32)
    twist_im = np.zeros((SLOT, LANES), np.float32)
    twist_re[:OUTER] = np.cos(twist)
    twist_im[:OUTER] = np.sin(twist)
    long = 2.0 * np.pi * ((lane[:, None] * lane[None, :]) % LANES) / LANES
    cos, sin = np.cos(long), np.sin(long)
    lanes = np.block([[cos, sin], [-sin, cos]])
    grid_h, grid_l = split_np(to_grid)
    modes_h, modes_l = split_np(to_modes)
    lanes_h, lanes_l = split_np(lanes)
    return dict(
        to_grid=np.concatenate([grid_h, grid_h, grid_l], axis=1),
        to_modes=np.concatenate([modes_h, modes_h, modes_l], axis=1),
        twist_re=twist_re,
        twist_im=twist_im,
        lanes_h=lanes_h,
        lanes_l=lanes_l,
    )


def dot(left, right):
    return jnp.dot(left, right, preferred_element_type=jnp.float32)


def split(value):
    high = value.astype(jnp.bfloat16)
    low = (value - high.astype(jnp.float32)).astype(jnp.bfloat16)
    return high, low


def load_modes(w_ref, field, row):
    base = field * PARTS + KEPT * row
    re = w_ref[pl.ds(base, 32), :]
    im = w_ref[pl.ds(base + PARTS // 2 - 2, 32), :]
    return jnp.concatenate([re, im], axis=0)


def lane_transform(high_ref, low_ref, lanes_h_ref, lanes_l_ref):
    table = lanes_h_ref[...]
    return (
        dot(high_ref[...], table) + dot(low_ref[...], table) + dot(high_ref[...], lanes_l_ref[...])
    )


def grid_kernel(w_ref, table_ref, twr_ref, twi_ref, lh_ref, ll_ref, out_ref, uh_ref, ul_ref):
    table = table_ref[...]
    twr, twi = twr_ref[...], twi_ref[...]
    for row in range(ROWS):
        modes = jnp.concatenate([load_modes(w_ref, 0, row), load_modes(w_ref, 1, row)], axis=1)
        high, low = split(modes)
        sums = dot(table, jnp.concatenate([high, low, high], axis=0))
        for field in range(2):
            lanes = slice(field * LANES, (field + 1) * LANES)
            re, im = sums[:SLOT, lanes], sums[SLOT:, lanes]
            twisted = jnp.concatenate([re * twr - im * twi, re * twi + im * twr], axis=1)
            high, low = split(twisted)
            rows = pl.ds((2 * row + field) * SLOT, SLOT)
            uh_ref[rows, :] = high
            ul_ref[rows, :] = low
    out_ref[...] = lane_transform(uh_ref, ul_ref, lh_ref, ll_ref)


def to_grid(own, tables):
    rows = 2 * ROWS * SLOT
    return pl.pallas_call(
        grid_kernel,
        out_shape=jax.ShapeDtypeStruct((rows, 2 * LANES), jnp.float32),
        scratch_shapes=[pltpu.VMEM((rows, 2 * LANES), jnp.bfloat16)] * 2,
        cost_estimate=pl.CostEstimate(
            flops=2 * rows * 256 * 256 * 3, bytes_accessed=1400000, transcendentals=0
        ),
        name="to_grid",
    )(
        own,
        tables["to_grid"],
        tables["twist_re"],
        tables["twist_im"],
        tables["lanes_h"],
        tables["lanes_l"],
    )


def pairs_of(x):
    return [(j ^ x, ((x - j) % 4) ^ x) for j in range(4)]


def complex_product(left, right):
    return (left[0] * right[0] - left[1] * right[1], left[0] * right[1] + left[1] * right[0])


def modes_kernel(
    x_ref, g0, g1, g2, g3, w_ref, mask_ref, table_ref, twr_ref, twi_ref, lh_ref, ll_ref,
    out_ref, uh_ref, ul_ref,
):
    grids = (g0, g1, g2, g3)
    x = x_ref[0]
    step_rows = 16

    def convolve(pairs):
        def step(index, carry):
            row = index // 3
            base = row * 2 * SLOT + (index - row * 3) * step_rows

            def load(grid, field):
                rows = pl.ds(pl.multiple_of(base + field * SLOT, step_rows), step_rows)
                return (grid[rows, pl.ds(0, LANES)], grid[rows, pl.ds(LANES, LANES)])

            a = [load(grid, 0) for grid in grids]
            b = [load(grid, 1) for grid in grids]
            p = q = None
            for left, right in pairs:
                ab = complex_product(a[left], b[right])
                aa = complex_product(a[left], a[right])
                bb = complex_product(b[left], b[right])
                if p is None:
                    p = ab
                    q = (aa[0] - bb[0], aa[1] - bb[1])
                else:
                    p = (p[0] + ab[0], p[1] + ab[1])
                    q = (q[0] + aa[0] - bb[0], q[1] + aa[1] - bb[1])
            for field, (re, im) in enumerate((p, q)):
                high, low = split(jnp.concatenate([re, -im], axis=1))
                rows = pl.ds(pl.multiple_of(base + field * SLOT, step_rows), step_rows)
                uh_ref[rows, :] = high
                ul_ref[rows, :] = low
            return carry

        lax.fori_loop(0, 3 * ROWS, step, 0)

    for value in range(4):

        @pl.when(x == value)
        def _(value=value):
            convolve(pairs_of(value))

    spectra = lane_transform(uh_ref, ul_ref, lh_ref, ll_ref)
    table = table_ref[...]
    twr, twi = twr_ref[...], twi_ref[...]
    mask = mask_ref[...]
    for row in range(ROWS):
        re_parts, im_parts = [], []
        for field in range(2):
            start = (2 * row + field) * SLOT
            re = spectra[start : start + SLOT, :LANES]
            im = spectra[start : start + SLOT, LANES:]
            re_parts.append(re * twr - im * twi)
            im_parts.append(re * twi + im * twr)
        twisted = jnp.concatenate(
            [jnp.concatenate(re_parts, axis=1), jnp.concatenate(im_parts, axis=1)], axis=0
        )
        high, low = split(twisted)
        hat = dot(table, jnp.concatenate([high, low, high], axis=0))
        columns = jnp.concatenate(
            [
                load_modes(w_ref, field, row)
                + hat[:, field * LANES : (field + 1) * LANES] * mask
                for field in range(2)
            ],
            axis=0,
        )
        out_ref[pl.ds(row, LANES, stride=ROWS), :] = columns.T


def to_rhs(x, grids, own, mask, tables):
    rows = 2 * ROWS * SLOT
    vmem = pl.BlockSpec(memory_space=pltpu.VMEM)
    return pl.pallas_call(
        modes_kernel,
        out_shape=jax.ShapeDtypeStruct((ROWS * LANES, LANES), jnp.float32),
        in_specs=[pl.BlockSpec(memory_space=pltpu.SMEM)] + [vmem] * 11,
        out_specs=vmem,
        scratch_shapes=[pltpu.VMEM((rows, 2 * LANES), jnp.bfloat16)] * 2,
        cost_estimate=pl.CostEstimate(
            flops=2 * rows * 256 * 256 * 3, bytes_accessed=3500000, transcendentals=0
        ),
        name="to_rhs",
    )(
        x,
        *grids,
        own,
        mask,
        tables["to_modes"],
        tables["twist_re"],
        tables["twist_im"],
        tables["lanes_h"],
        tables["lanes_l"],
    )


def matmul3(left, right, contract=((1,), (0,))):
    left_h, left_l = split(left)
    right_h, right_l = split(right)

    def one(u, v):
        return lax.dot_general(u, v, (contract, ((), ())), preferred_element_type=jnp.float32)

    return one(left_h, right_h) + one(left_h, right_l) + one(left_l, right_h)


def operator_kernel(inv_ref, mult_ref, high_ref, low_ref, g_ref, s_ref):
    nblocks, width, _ = inv_ref.shape
    eye = (
        lax.broadcasted_iota(jnp.int32, (width, width), 0)
        == lax.broadcasted_iota(jnp.int32, (width, width), 1)
    ).astype(jnp.float32)
    for j in range(nblocks):
        rows = pl.ds(j * width, width)
        if j:
            g_ref[rows, : j * width] = -matmul3(
                mult_ref[j - 1], g_ref[pl.ds((j - 1) * width, width), : j * width]
            )
        g_ref[rows, j * width : (j + 1) * width] = eye
    for j in reversed(range(nblocks)):
        rows = pl.ds(j * width, width)
        own = (j + 1) * width
        result = matmul3(inv_ref[j], g_ref[rows, :own])
        if j < nblocks - 1:
            result = jnp.concatenate(
                [result, jnp.zeros((width, (nblocks - 1 - j) * width), jnp.float32)], axis=1
            )
            result = result - matmul3(
                mult_ref[j], s_ref[pl.ds((j + 1) * width, width), :], ((0,), (0,))
            )
        s_ref[rows, :] = result
        high, low = split(result)
        high_ref[rows, :] = high
        low_ref[rows, :] = low


def solve_operator(block_inv, lower_mult):
    size = block_inv.shape[0] * block_inv.shape[1]
    return pl.pallas_call(
        operator_kernel,
        out_shape=[jax.ShapeDtypeStruct((size, size), jnp.bfloat16)] * 2,
        scratch_shapes=[pltpu.VMEM((size, size), jnp.float32)] * 2,
        cost_estimate=pl.CostEstimate(
            flops=2 * 55 * 3 * 128**3 * 4, bytes_accessed=3100000, transcendentals=0
        ),
        name="solve_operator",
    )(block_inv, lower_mult)


def solve_kernel(high_ref, low_ref, r_ref, out_ref):
    high, low = split(r_ref[...])
    both = dot(high_ref[...], jnp.concatenate([high, low], axis=1))
    out_ref[...] = both[:, :LANES] + both[:, LANES:] + dot(low_ref[...], high)


def solve(operator, rhs):
    return pl.pallas_call(
        solve_kernel,
        out_shape=jax.ShapeDtypeStruct(rhs.shape, jnp.float32),
        name="solve",
    )(*operator, rhs)


def spread_kernel(s_ref, a_ref, b_ref):
    for row in range(ROWS):
        columns = s_ref[pl.ds(row, LANES, stride=ROWS), :].T
        for field, ref in enumerate((a_ref, b_ref)):
            base = field * 64
            ref[pl.ds(row * KEPT, KEPT), :] = columns[base : base + KEPT]
            ref[pl.ds(PARTS // 2 + row * KEPT, KEPT), :] = columns[base + 34 : base + 64]


def spread(solved):
    return pl.pallas_call(
        spread_kernel,
        out_shape=[jax.ShapeDtypeStruct((PARTS, LANES), jnp.float32)] * 2,
        name="spread",
    )(solved)


def exchange(rows):
    count = rows.shape[0] // ROWS
    sent = rows.reshape(count, 1, ROWS * LANES)
    return lax.all_to_all(sent, "wa", 0, 0, tiled=True).reshape(rows.shape)


def permute(value, flip):
    return lax.ppermute(value, "gx", [(i, i ^ flip) for i in range(4)])


def body(field_a, field_b, keep_mask, block_inv, lower_mult):
    tables = {name: jnp.asarray(table) for name, table in build_tables().items()}
    own = jnp.concatenate([field_a.reshape(PARTS, LANES), field_b.reshape(PARTS, LANES)], axis=0)
    keep = keep_mask.astype(jnp.float32).reshape(KEPT, LANES)
    gap = jnp.zeros((2, LANES), jnp.float32)
    mask = jnp.concatenate([keep, gap, gap, keep], axis=0)
    x = lax.axis_index("gx").astype(jnp.int32).reshape(1)

    two = permute(own, 2)
    one = permute(own, 1)
    three = permute(two, 1)
    operator = solve_operator(block_inv, lower_mult)
    grids = [to_grid(part, tables) for part in (own, one, two, three)]
    rhs = to_rhs(x, grids, own, mask, tables)
    solved = solve(operator, exchange(rhs))
    new_a, new_b = spread(exchange(solved))
    return (new_a.reshape(field_a.shape), new_b.reshape(field_b.shape))


def solution(mesh):
    return jax.shard_map(
        body,
        mesh=mesh,
        in_specs=(P(None, "gx", "wa", None), P(None, "gx", "wa", None), P(), P(), P()),
        out_specs=(P(None, "gx", "wa", None), P(None, "gx", "wa", None)),
        check_vma=False,
    )
```

profile of v0, /device:TPU:6, one launch (start us, length us, event | category | flops | bytes accessed | tf_op | source)
XLA Modules:
  0.0 127.3 jit_solution(4026693675270112118)
XLA Ops:
  0.6 1.0 pad_maximum_fusion.w_ref
  1.7 0.0 copy-start
  1.7 3.5 %collective-permute-start.1 = (f32[720,128]{1,0:T(8,128)S(1)}, f32[720,128]{1,0:T(8,128)S(1)}, u32[]{:S(2)}, u32[]{:S(2)}) collective-permute-start(f32[720,128]{1,0:T(8,128)S(1)} %pad_maximum_fusion.w_ref), channel_id=1, source_target_pairs={{0,2},{1,3},{2,0},{3,1},{4,6},{5,7},{6,4},{7,5},{8,10},{9,11},{10,... | collective-permute-start | bytes 1105928 | tf_op jit(solution)/shard_map/ppermute | solution.py:330
  5.2 1.9 %collective-permute-start = (f32[720,128]{1,0:T(8,128)S(1)}, f32[720,128]{1,0:T(8,128)S(1)}, u32[]{:S(2)}, u32[]{:S(2)}) collective-permute-start(f32[720,128]{1,0:T(8,128)S(1)} %pad_maximum_fusion.w_ref), channel_id=1, source_target_pairs={{0,1},{1,0},{2,3},{3,2},{4,5},{5,4},{6,7},{7,6},{8,9},{9,8},{10,11... | collective-permute-start | bytes 1105928 | tf_op jit(solution)/shard_map/ppermute | solution.py:330
  7.1 6.8 %collective-permute-done.1.w_ref = f32[720,128]{1,0:T(8,128)S(1)} collective-permute-done((f32[720,128]{1,0:T(8,128)S(1)}, f32[720,128]{1,0:T(8,128)S(1)}, u32[]{:S(2)}, u32[]{:S(2)}) %collective-permute-start.1) | collective-permute-done | bytes 368672 | tf_op jit(solution)/shard_map/ppermute | solution.py:330
  13.9 0.0 copy-start.2
  13.9 1.9 %collective-permute-start.2 = (f32[720,128]{1,0:T(8,128)S(1)}, f32[720,128]{1,0:T(8,128)S(1)}, u32[]{:S(2)}, u32[]{:S(2)}) collective-permute-start(f32[720,128]{1,0:T(8,128)S(1)} %collective-permute-done.1.w_ref), channel_id=1, source_target_pairs={{0,1},{1,0},{2,3},{3,2},{4,5},{5,4},{6,7},{7,6},{8,9},{9,8},{10,11... | collective-permute-start | bytes 1105928 | tf_op jit(solution)/shard_map/ppermute | solution.py:330
  15.8 0.7 convert_bitcast_fusion
  16.5 0.1 pad.1.clone
  16.6 0.0 copy-done
  16.6 2.5 %to_grid.4.g0 = f32[576,256]{1,0:T(8,128)} custom-call(f32[720,128]{1,0:T(8,128)} %copy-done, bf16[96,192]{1,0:T(8,128)(2,1)} %constant.18.clone.table_ref, f32[48,128]{1,0:T(8,128)} %constant.20.clone.twr_ref, f32[48,128]{1,0:T(8,128)} %constant.21.clone.twi_ref, bf16[256,256]{1,0:T(8,128)(2,1)} %constant.22.clone.lh_ref, ...), custom_call_target="tpu_custom_call" | custom-call | flops 226492416 | bytes 1400000 | tf_op jit(solution)/shard_map/to_grid/pallas_call | solution.py:114
  19.1 0.7 pad_maximum_fusion.1.mask_ref
  19.8 0.0 copy-done.2
  19.8 2.5 %to_grid.6.g2 = f32[576,256]{1,0:T(8,128)} custom-call(f32[720,128]{1,0:T(8,128)} %copy-done.2, bf16[96,192]{1,0:T(8,128)(2,1)} %constant.18.clone.table_ref, f32[48,128]{1,0:T(8,128)} %constant.20.clone.twr_ref, f32[48,128]{1,0:T(8,128)} %constant.21.clone.twi_ref, bf16[256,256]{1,0:T(8,128)(2,1)} %constant.22.clone.lh_ref, ...), custom_call_target="tpu_custom_call" | custom-call | flops 226492416 | bytes 1400000 | tf_op jit(solution)/shard_map/to_grid/pallas_call | solution.py:114
  22.3 0.0 collective-permute-done.w_ref
  22.3 0.0 copy-start.3
  22.4 0.8 copy-done.3
  23.1 2.5 %to_grid.5.g1 = f32[576,256]{1,0:T(8,128)} custom-call(f32[720,128]{1,0:T(8,128)} %copy-done.3, bf16[96,192]{1,0:T(8,128)(2,1)} %constant.18.clone.table_ref, f32[48,128]{1,0:T(8,128)} %constant.20.clone.twr_ref, f32[48,128]{1,0:T(8,128)} %constant.21.clone.twi_ref, bf16[256,256]{1,0:T(8,128)(2,1)} %constant.22.clone.lh_ref, ...), custom_call_target="tpu_custom_call" | custom-call | flops 226492416 | bytes 1400000 | tf_op jit(solution)/shard_map/to_grid/pallas_call | solution.py:114
  25.6 0.0 collective-permute-done.2.w_ref
  25.6 0.0 copy-start.4
  25.6 0.7 copy-done.4
  26.4 2.5 %to_grid.7.g3 = f32[576,256]{1,0:T(8,128)} custom-call(f32[720,128]{1,0:T(8,128)} %copy-done.4, bf16[96,192]{1,0:T(8,128)(2,1)} %constant.18.clone.table_ref, f32[48,128]{1,0:T(8,128)} %constant.20.clone.twr_ref, f32[48,128]{1,0:T(8,128)} %constant.21.clone.twi_ref, bf16[256,256]{1,0:T(8,128)(2,1)} %constant.22.clone.lh_ref, ...), custom_call_target="tpu_custom_call" | custom-call | flops 226492416 | bytes 1400000 | tf_op jit(solution)/shard_map/to_grid/pallas_call | solution.py:114
  28.9 4.3 %to_rhs.1 = f32[768,128]{1,0:T(8,128)} custom-call(s32[1]{0:T(128)} %bitcast.x_ref, f32[576,256]{1,0:T(8,128)} %to_grid.4.g0, f32[576,256]{1,0:T(8,128)} %to_grid.5.g1, f32[576,256]{1,0:T(8,128)} %to_grid.6.g2, f32[576,256]{1,0:T(8,128)} %to_grid.7.g3, f32[720,128]{1,0:T(8,128)} %copy-done, f32[64,128]{1,0:T(8,128)} %pad_maximum_fusion.1.mask_ref, ...), custom_call_target="tpu_custom_call" | custom-call | flops 226492416 | bytes 3500000 | tf_op jit(solution)/shard_map/to_rhs/pallas_call | solution.py:216
  33.2 22.0 %all-to-all-start = ((f32[128,1,768]{2,1,0:T(1,128)}), f32[128,1,768]{2,1,0:T(1,128)S(1)}, u32[]{:S(2)}, u32[]{:S(2)}) async-start(f32[128,1,768]{2,1,0:T(1,128)} %bitcast.11), calls=%async_computation | async-start | bytes 786432 | tf_op jit(solution)/shard_map/all_to_all | solution.py:326
  55.2 5.7 %solve_operator.1 = (bf16[768,768]{1,0:T(8,128)(2,1)}, bf16[768,768]{1,0:T(8,128)(2,1)}) custom-call(f32[6,128,128]{2,1,0:T(8,128)} %inv_ref.1, f32[5,128,128]{2,1,0:T(8,128)} %mult_ref.1), custom_call_target="tpu_custom_call" | custom-call | flops 2768240640 | bytes 3100000 | tf_op jit(solution)/shard_map/solve_operator/pallas_call | solution.py:281
  60.9 24.8 %all-to-all-done = f32[128,1,768]{2,1,0:T(1,128)S(1)} async-done(((f32[128,1,768]{2,1,0:T(1,128)}), f32[128,1,768]{2,1,0:T(1,128)S(1)}, u32[]{:S(2)}, u32[]{:S(2)}) %all-to-all-start) | async-done | bytes 393248 | tf_op jit(solution)/shard_map/all_to_all | solution.py:326
  85.7 0.0 copy-start.1
  85.8 0.8 copy-done.1
  86.5 3.2 %solve.1 = f32[768,128]{1,0:T(8,128)} custom-call(bf16[768,768]{1,0:T(8,128)(2,1)} %get-tuple-element.6.high_ref, bf16[768,768]{1,0:T(8,128)(2,1)} %get-tuple-element.7.low_ref, f32[768,128]{1,0:T(8,128)} %bitcast.12), custom_call_target="tpu_custom_call" | custom-call | tf_op jit(solution)/shard_map/solve/pallas_call | solution.py:299
  89.7 35.7 %all_to_all.10 = f32[128,1,768]{2,1,0:T(1,128)} all-to-all(f32[128,1,768]{2,1,0:T(1,128)} %bitcast.13), channel_id=1, replica_groups=mesh['wa'=128,'gx'=4] {'wa'}, dimensions={0} | all-to-all | bytes 786432 | tf_op jit(solution)/shard_map/all_to_all | solution.py:326
  125.4 1.9 %spread.1 = (f32[360,128]{1,0:T(8,128)}, f32[360,128]{1,0:T(8,128)}) custom-call(f32[768,128]{1,0:T(8,128)} %bitcast.14), custom_call_target="tpu_custom_call" | custom-call | tf_op jit(solution)/shard_map/spread/pallas_call | solution.py:316
  (1 shorter events, 0.0 us)
Async XLA Ops:
  1.7 15.0 %copy-start = (f32[720,128]{1,0:T(8,128)}, f32[720,128]{1,0:T(8,128)S(1)}, u32[]{:S(2)}) copy-start(f32[720,128]{1,0:T(8,128)S(1)} %pad_maximum_fusion.w_ref) | copy-start | bytes 1105924
  1.7 12.2 %collective-permute-start.1 = (f32[720,128]{1,0:T(8,128)S(1)}, f32[720,128]{1,0:T(8,128)S(1)}, u32[]{:S(2)}, u32[]{:S(2)}) collective-permute-start(f32[720,128]{1,0:T(8,128)S(1)} %pad_maximum_fusion.w_ref), channel_id=1, source_target_pairs={{0,2},{1,3},{2,0},{3,1},{4,6},{5,7},{6,4},{7,5},{8,10},{9,11},{10,... | collective-permute-start | bytes 1105928 | tf_op jit(solution)/shard_map/ppermute | solution.py:330
  5.2 17.2 %collective-permute-start = (f32[720,128]{1,0:T(8,128)S(1)}, f32[720,128]{1,0:T(8,128)S(1)}, u32[]{:S(2)}, u32[]{:S(2)}) collective-permute-start(f32[720,128]{1,0:T(8,128)S(1)} %pad_maximum_fusion.w_ref), channel_id=1, source_target_pairs={{0,1},{1,0},{2,3},{3,2},{4,5},{5,4},{6,7},{7,6},{8,9},{9,8},{10,11... | collective-permute-start | bytes 1105928 | tf_op jit(solution)/shard_map/ppermute | solution.py:330
  13.9 5.9 %copy-start.2 = (f32[720,128]{1,0:T(8,128)}, f32[720,128]{1,0:T(8,128)S(1)}, u32[]{:S(2)}) copy-start(f32[720,128]{1,0:T(8,128)S(1)} %collective-permute-done.1.w_ref) | copy-start | bytes 1105924
  13.9 11.7 %collective-permute-start.2 = (f32[720,128]{1,0:T(8,128)S(1)}, f32[720,128]{1,0:T(8,128)S(1)}, u32[]{:S(2)}, u32[]{:S(2)}) collective-permute-start(f32[720,128]{1,0:T(8,128)S(1)} %collective-permute-done.1.w_ref), channel_id=1, source_target_pairs={{0,1},{1,0},{2,3},{3,2},{4,5},{5,4},{6,7},{7,6},{8,9},{9,8},{10,11... | collective-permute-start | bytes 1105928 | tf_op jit(solution)/shard_map/ppermute | solution.py:330
  22.3 0.8 copy-start.3
  25.6 0.7 copy-start.4
  33.2 52.6 %all-to-all-start = ((f32[128,1,768]{2,1,0:T(1,128)}), f32[128,1,768]{2,1,0:T(1,128)S(1)}, u32[]{:S(2)}, u32[]{:S(2)}) async-start(f32[128,1,768]{2,1,0:T(1,128)} %bitcast.11), calls=%async_computation | async-start | bytes 786432 | tf_op jit(solution)/shard_map/all_to_all | solution.py:326
  85.7 0.8 copy-start.1
where the time goes:
time: 128 us; the launch traced here: 127 us
  blocking collectives  35.7 us (28%)
  waiting for transfers between devices  31.6 us (25%)
  starting transfers between devices  29.3 us (23%)
  Pallas kernels  25.2 us (20%)
  other arithmetic  2.45 us (2%)
  local copies, waits for them, and re-layouts  2.34 us (2%)
    all_to_all x1, blocking collectives, exchange(): return lax.all_to_all(sent, 'wa', 0, 0, tiled=True).reshape(rows.shape)  35.7 us
    all_to_all x1, waiting for transfers between devices, exchange(): return lax.all_to_all(sent, 'wa', 0, 0, tiled=True).reshape(rows.shape)  24.8 us
    all_to_all x1, starting transfers between devices, exchange(): return lax.all_to_all(sent, 'wa', 0, 0, tiled=True).reshape(rows.shape)  22 us
    pallas_call x4, Pallas kernels, to_grid(): pl.pallas_call(grid_kernel, out_shape=jax.ShapeDtypeStruct((rows, 2 * LAN...  10.1 us
    ppermute x3, starting transfers between devices, permute(): return lax.ppermute(value, 'gx', [(i, i ^ flip) for i in range(4)])  7.31 us
    ppermute x3, waiting for transfers between devices, permute(): return lax.ppermute(value, 'gx', [(i, i ^ flip) for i in range(4)])  6.81 us
    pallas_call x1, Pallas kernels, solve_operator(): pl.pallas_call(operator_kernel, out_shape=[jax.ShapeDtypeStruct((size, si...  5.72 us
    pallas_call x1, Pallas kernels, to_rhs(): pl.pallas_call(modes_kernel, out_shape=jax.ShapeDtypeStruct((ROWS * LANES...  4.3 us
  transfers between devices with their start and end apart: 4, of which 2 were waited for; matrix products, arithmetic and copies ran while one was open for 1% of the time, Pallas kernels for 10%

commit v1 on v0

--- a/solution.py
+++ b/solution.py
@@ -7,6 +7,7 @@
 from jax import lax
 from jax.experimental import pallas as pl
 from jax.experimental.pallas import tpu as pltpu
+from jax.sharding import Mesh
 from jax.sharding import PartitionSpec as P
 
 NL_COEFF = 0.25
@@ -16,7 +17,9 @@
 OUTER = 45
 KEPT = 30
 ROWS = 6
+HALF = ROWS // 2
 SLOT = 48
+PADDED = 64
 PARTS = 2 * ROWS * KEPT
 
 
@@ -77,11 +80,31 @@
     return high, low
 
 
-def load_modes(w_ref, field, row):
-    base = field * PARTS + KEPT * row
-    re = w_ref[pl.ds(base, 32), :]
-    im = w_ref[pl.ds(base + PARTS // 2 - 2, 32), :]
-    return jnp.concatenate([re, im], axis=0)
+def prepare_kernel(y_ref, a_ref, b_ref, send_ref, keep_ref):
+    mine = y_ref[0]
+    for half, out_ref in ((1 - mine, send_ref), (mine, keep_ref)):
+        for field, ref in enumerate((a_ref, b_ref)):
+            for i in range(HALF):
+                base = half * (HALF * KEPT) + i * KEPT
+                row = (field * HALF + i) * PADDED
+                out_ref[pl.ds(row, 32), :] = ref[pl.ds(base, 32), :]
+                out_ref[pl.ds(row + 32, 32), :] = ref[pl.ds(base + PARTS // 2 - 2, 32), :]
+
+
+def prepare(y, field_a, field_b):
+    vmem = pl.BlockSpec(memory_space=pltpu.VMEM)
+    shape = jax.ShapeDtypeStruct((2 * HALF * PADDED, LANES), jnp.float32)
+    return pl.pallas_call(
+        prepare_kernel,
+        out_shape=[shape, shape],
+        in_specs=[pl.BlockSpec(memory_space=pltpu.SMEM), vmem, vmem],
+        out_specs=[vmem, vmem],
+        name="prepare",
+    )(y, field_a, field_b)
+
+
+def load_modes(w_ref, field, i):
+    return w_ref[pl.ds((field * HALF + i) * PADDED, PADDED), :]
 
 
 def lane_transform(high_ref, low_ref, lanes_h_ref, lanes_l_ref):
@@ -94,7 +117,7 @@
 def grid_kernel(w_ref, table_ref, twr_ref, twi_ref, lh_ref, ll_ref, out_ref, uh_ref, ul_ref):
     table = table_ref[...]
     twr, twi = twr_ref[...], twi_ref[...]
-    for row in range(ROWS):
+    for row in range(HALF):
         modes = jnp.concatenate([load_modes(w_ref, 0, row), load_modes(w_ref, 1, row)], axis=1)
         high, low = split(modes)
         sums = dot(table, jnp.concatenate([high, low, high], axis=0))
@@ -110,13 +133,13 @@
 
 
 def to_grid(own, tables):
-    rows = 2 * ROWS * SLOT
+    rows = 2 * HALF * SLOT
     return pl.pallas_call(
         grid_kernel,
         out_shape=jax.ShapeDtypeStruct((rows, 2 * LANES), jnp.float32),
         scratch_shapes=[pltpu.VMEM((rows, 2 * LANES), jnp.bfloat16)] * 2,
         cost_estimate=pl.CostEstimate(
-            flops=2 * rows * 256 * 256 * 3, bytes_accessed=1400000, transcendentals=0
+            flops=2 * rows * 256 * 256 * 3, bytes_accessed=900000, transcendentals=0
         ),
         name="to_grid",
     )(
@@ -129,8 +152,8 @@
     )
 
 
-def pairs_of(x):
-    return [(j ^ x, ((x - j) % 4) ^ x) for j in range(4)]
+def pairs_of(x, target):
+    return [(j ^ x, ((target - j) % 4) ^ x) for j in range(4)]
 
 
 def complex_product(left, right):
@@ -138,17 +161,18 @@
 
 
 def modes_kernel(
-    x_ref, g0, g1, g2, g3, w_ref, mask_ref, table_ref, twr_ref, twi_ref, lh_ref, ll_ref,
+    x_ref, g0, g1, g2, g3, w0_ref, w2_ref, mask_ref, table_ref, twr_ref, twi_ref, lh_ref, ll_ref,
     out_ref, uh_ref, ul_ref,
 ):
     grids = (g0, g1, g2, g3)
     x = x_ref[0]
     step_rows = 16
 
-    def convolve(pairs):
+    def convolve(all_pairs):
         def step(index, carry):
             row = index // 3
-            base = row * 2 * SLOT + (index - row * 3) * step_rows
+            part = (index - row * 3) * step_rows
+            base = row * 2 * SLOT + part
 
             def load(grid, field):
                 rows = pl.ds(pl.multiple_of(base + field * SLOT, step_rows), step_rows)
@@ -156,31 +180,33 @@
 
             a = [load(grid, 0) for grid in grids]
             b = [load(grid, 1) for grid in grids]
-            p = q = None
-            for left, right in pairs:
-                ab = complex_product(a[left], b[right])
-                aa = complex_product(a[left], a[right])
-                bb = complex_product(b[left], b[right])
-                if p is None:
-                    p = ab
-                    q = (aa[0] - bb[0], aa[1] - bb[1])
-                else:
-                    p = (p[0] + ab[0], p[1] + ab[1])
-                    q = (q[0] + aa[0] - bb[0], q[1] + aa[1] - bb[1])
-            for field, (re, im) in enumerate((p, q)):
-                high, low = split(jnp.concatenate([re, -im], axis=1))
-                rows = pl.ds(pl.multiple_of(base + field * SLOT, step_rows), step_rows)
-                uh_ref[rows, :] = high
-                ul_ref[rows, :] = low
+            for target, pairs in enumerate(all_pairs):
+                p = q = None
+                for left, right in pairs:
+                    ab = complex_product(a[left], b[right])
+                    aa = complex_product(a[left], a[right])
+                    bb = complex_product(b[left], b[right])
+                    if p is None:
+                        p = ab
+                        q = (aa[0] - bb[0], aa[1] - bb[1])
+                    else:
+                        p = (p[0] + ab[0], p[1] + ab[1])
+                        q = (q[0] + aa[0] - bb[0], q[1] + aa[1] - bb[1])
+                for field, (re, im) in enumerate((p, q)):
+                    high, low = split(jnp.concatenate([re, -im], axis=1))
+                    start = base + (target * 2 * HALF + field) * SLOT
+                    rows = pl.ds(pl.multiple_of(start, step_rows), step_rows)
+                    uh_ref[rows, :] = high
+                    ul_ref[rows, :] = low
             return carry
 
-        lax.fori_loop(0, 3 * ROWS, step, 0)
+        lax.fori_loop(0, 3 * HALF, step, 0)
 
     for value in range(4):
 
         @pl.when(x == value)
         def _(value=value):
-            convolve(pairs_of(value))
+            convolve([pairs_of(value, 2 * target + value % 2) for target in range(2)])
 
     spectra = lane_transform(uh_ref, ul_ref, lh_ref, ll_ref)
     table = table_ref[...]
@@ -199,9 +225,14 @@
         )
         high, low = split(twisted)
         hat = dot(table, jnp.concatenate([high, low, high], axis=0))
+        mine = (x // 2) == row // HALF
         columns = jnp.concatenate(
             [
-                load_modes(w_ref, field, row)
+                jnp.where(
+                    mine,
+                    load_modes(w0_ref, field, row % HALF),
+                    load_modes(w2_ref, field, row % HALF),
+                )
                 + hat[:, field * LANES : (field + 1) * LANES] * mask
                 for field in range(2)
             ],
@@ -210,23 +241,24 @@
         out_ref[pl.ds(row, LANES, stride=ROWS), :] = columns.T
 
 
-def to_rhs(x, grids, own, mask, tables):
+def to_rhs(x, grids, own, other, mask, tables):
     rows = 2 * ROWS * SLOT
     vmem = pl.BlockSpec(memory_space=pltpu.VMEM)
     return pl.pallas_call(
         modes_kernel,
         out_shape=jax.ShapeDtypeStruct((ROWS * LANES, LANES), jnp.float32),
-        in_specs=[pl.BlockSpec(memory_space=pltpu.SMEM)] + [vmem] * 11,
+        in_specs=[pl.BlockSpec(memory_space=pltpu.SMEM)] + [vmem] * 12,
         out_specs=vmem,
         scratch_shapes=[pltpu.VMEM((rows, 2 * LANES), jnp.bfloat16)] * 2,
         cost_estimate=pl.CostEstimate(
-            flops=2 * rows * 256 * 256 * 3, bytes_accessed=3500000, transcendentals=0
+            flops=2 * rows * 256 * 256 * 3, bytes_accessed=2400000, transcendentals=0
         ),
         name="to_rhs",
     )(
         x,
         *grids,
         own,
+        other,
         mask,
         tables["to_modes"],
         tables["twist_re"],
@@ -289,16 +321,28 @@
     )(block_inv, lower_mult)
 
 
-def solve_kernel(high_ref, low_ref, r_ref, out_ref):
-    high, low = split(r_ref[...])
-    both = dot(high_ref[...], jnp.concatenate([high, low], axis=1))
-    out_ref[...] = both[:, :LANES] + both[:, LANES:] + dot(low_ref[...], high)
+def solve_kernel(high_ref, low_ref, r_ref, out_ref, rh_ref):
+    @pl.when(pl.program_id(0) == 0)
+    def _():
+        high, low = split(r_ref[...])
+        rh_ref[:, :LANES] = high
+        rh_ref[:, LANES:] = low
+
+    both = dot(high_ref[...], rh_ref[...])
+    out_ref[...] = both[:, :LANES] + both[:, LANES:] + dot(low_ref[...], rh_ref[:, :LANES])
 
 
 def solve(operator, rhs):
+    size = rhs.shape[0]
+    steps = 3
+    blocks = pl.BlockSpec((size // steps, size), lambda i: (i, 0))
     return pl.pallas_call(
         solve_kernel,
         out_shape=jax.ShapeDtypeStruct(rhs.shape, jnp.float32),
+        grid=(steps,),
+        in_specs=[blocks, blocks, pl.BlockSpec((size, LANES), lambda i: (0, 0))],
+        out_specs=pl.BlockSpec((size // steps, LANES), lambda i: (i, 0)),
+        scratch_shapes=[pltpu.VMEM((size, 2 * LANES), jnp.bfloat16)],
         name="solve",
     )(*operator, rhs)
 
@@ -320,40 +364,45 @@
     )(solved)
 
 
-def exchange(rows):
-    count = rows.shape[0] // ROWS
-    sent = rows.reshape(count, 1, ROWS * LANES)
-    return lax.all_to_all(sent, "wa", 0, 0, tiled=True).reshape(rows.shape)
-
-
-def permute(value, flip):
-    return lax.ppermute(value, "gx", [(i, i ^ flip) for i in range(4)])
+def exchange(rows, axes, count):
+    sent = rows.reshape(count, 1, ROWS * LANES * LANES // count)
+    return lax.all_to_all(sent, axes, 0, 0, tiled=True).reshape(rows.shape)
+
+
+def swap(value, axis):
+    return lax.ppermute(value, axis, [(0, 1), (1, 0)])
 
 
 def body(field_a, field_b, keep_mask, block_inv, lower_mult):
     tables = {name: jnp.asarray(table) for name, table in build_tables().items()}
-    own = jnp.concatenate([field_a.reshape(PARTS, LANES), field_b.reshape(PARTS, LANES)], axis=0)
+    y = lax.axis_index("y").astype(jnp.int32).reshape(1)
+    x = 2 * y + lax.axis_index("c").astype(jnp.int32)
+    send, own = prepare(y, field_a.reshape(PARTS, LANES), field_b.reshape(PARTS, LANES))
+    two = swap(send, "y")
+    one = swap(own, "c")
+    grids = [to_grid(own, tables), to_grid(one, tables)]
+    two, *grids = lax.optimization_barrier((two, *grids))
+    three = swap(two, "c")
+    grids += [to_grid(two, tables), to_grid(three, tables)]
+
     keep = keep_mask.astype(jnp.float32).reshape(KEPT, LANES)
     gap = jnp.zeros((2, LANES), jnp.float32)
     mask = jnp.concatenate([keep, gap, gap, keep], axis=0)
-    x = lax.axis_index("gx").astype(jnp.int32).reshape(1)
-
-    two = permute(own, 2)
-    one = permute(own, 1)
-    three = permute(two, 1)
+    rhs = to_rhs(x, grids, own, two, mask, tables)
     operator = solve_operator(block_inv, lower_mult)
-    grids = [to_grid(part, tables) for part in (own, one, two, three)]
-    rhs = to_rhs(x, grids, own, mask, tables)
-    solved = solve(operator, exchange(rhs))
-    new_a, new_b = spread(exchange(solved))
+    solved = solve(operator, exchange(rhs, ("wa", "y"), 256))
+    new_a, new_b = spread(exchange(solved, "wa", 128))
     return (new_a.reshape(field_a.shape), new_b.reshape(field_b.shape))
 
 
 def solution(mesh):
+    wa, gx = mesh.devices.shape
+    fine = Mesh(mesh.devices.reshape(wa, 2, gx // 2), ("wa", "y", "c"))
+    fields = P(None, ("y", "c"), "wa", None)
     return jax.shard_map(
         body,
-        mesh=mesh,
-        in_specs=(P(None, "gx", "wa", None), P(None, "gx", "wa", None), P(), P(), P()),
-        out_specs=(P(None, "gx", "wa", None), P(None, "gx", "wa", None)),
+        mesh=fine,
+        in_specs=(fields, fields, P(), P(), P()),
+        out_specs=(fields, fields),
         check_vma=False,
     )

time: 128 us -> 121 us (0.945)
  waiting for transfers between devices: 31.6 us -> 22.3 us
  other arithmetic: 2.45 us -> 0.69 us
  starting transfers between devices: 29.3 us -> 31 us
  blocking collectives: 35.7 us -> 37 us
    ppermute x3, waiting for transfers between devices: 6.81 us -> 0.01 us  [swap(): return lax.ppermute(value, axis, [(0, 1), (1, 0)])]
    all_to_all x1, waiting for transfers between devices: 24.8 us -> 22.3 us  [exchange(): return lax.all_to_all(sent, axes, 0, 0, tiled=True).reshape(rows.shape)]
    pallas_call x0 -> x1, Pallas kernels: none -> 1.82 us  [prepare(): pl.pallas_call(prepare_kernel, out_shape=[shape, shape], in_specs=[pl.Blo...]
    all_to_all x1, blocking collectives: 35.7 us -> 37 us  [exchange(): return lax.all_to_all(sent, axes, 0, 0, tiled=True).reshape(rows.shape)]
  transfers between devices with their start and end apart: 4 -> 4, of which waited for: 2 -> 1; matrix products, arithmetic and copies ran while one was open for 1% -> 1% of each run, Pallas kernels for 10% -> 10%
where the time goes in v1:
time: 121 us; the launch traced here: 120 us
  blocking collectives  37 us (31%)
  starting transfers between devices  31 us (26%)
  Pallas kernels  26.2 us (22%)
  waiting for transfers between devices  22.3 us (18%)
  local copies, waits for them, and re-layouts  2.2 us (2%)
    all_to_all x1, blocking collectives, exchange(): return lax.all_to_all(sent, axes, 0, 0, tiled=True).reshape(rows.shape)  37 us
    all_to_all x1, starting transfers between devices, exchange(): return lax.all_to_all(sent, axes, 0, 0, tiled=True).reshape(rows.shape)  23.2 us
    all_to_all x1, waiting for transfers between devices, exchange(): return lax.all_to_all(sent, axes, 0, 0, tiled=True).reshape(rows.shape)  22.3 us
    pallas_call x4, Pallas kernels, to_grid(): pl.pallas_call(grid_kernel, out_shape=jax.ShapeDtypeStruct((rows, 2 * LAN...  9.12 us
    ppermute x3, starting transfers between devices, swap(): return lax.ppermute(value, axis, [(0, 1), (1, 0)])  7.79 us
    pallas_call x1, Pallas kernels, solve_operator(): pl.pallas_call(operator_kernel, out_shape=[jax.ShapeDtypeStruct((size, si...  5.73 us
    pallas_call x1, Pallas kernels, solve(): pl.pallas_call(solve_kernel, out_shape=jax.ShapeDtypeStruct(rhs.shape, jn...  3.87 us
    pallas_call x1, Pallas kernels, to_rhs(): pl.pallas_call(modes_kernel, out_shape=jax.ShapeDtypeStruct((ROWS * LANES...  3.76 us
  transfers between devices with their start and end apart: 4, of which 1 were waited for; matrix products, arithmetic and copies ran while one was open for 1% of the time, Pallas kernels for 10%

profile of v1, /device:TPU:6, one launch (start us, length us, event | category | flops | bytes accessed | tf_op | source)
XLA Modules:
  0.0 120.1 jit_solution(11696920799176347332)
XLA Ops:
  0.6 0.0 copy-start.4
  0.6 1.8 %prepare.1 = (f32[384,128]{1,0:T(8,128)}, f32[384,128]{1,0:T(8,128)}) custom-call(s32[1]{0:T(128)} %bitcast.y_ref, f32[360,128]{1,0:T(8,128)} %bitcast.16, f32[360,128]{1,0:T(8,128)} %bitcast.17), custom_call_target="tpu_custom_call" | custom-call | tf_op jit(solution)/shard_map/prepare/pallas_call | solution.py:97
  2.5 3.5 %collective-permute-start = (f32[384,128]{1,0:T(8,128)}, f32[384,128]{1,0:T(8,128)S(1)}, u32[]{:S(2)}, u32[]{:S(2)}) collective-permute-start(f32[384,128]{1,0:T(8,128)} %get-tuple-element.13), channel_id=1, source_target_pairs={{0,2},{2,0},{1,3},{3,1},{4,6},{6,4},{5,7},{7,5},{8,10},{10,8},{9,1... | collective-permute-start | bytes 589832 | tf_op jit(solution)/shard_map/ppermute | solution.py:373
  5.9 1.9 %collective-permute-start.1 = (f32[384,128]{1,0:T(8,128)}, f32[384,128]{1,0:T(8,128)S(1)}, u32[]{:S(2)}, u32[]{:S(2)}) collective-permute-start(f32[384,128]{1,0:T(8,128)} %get-tuple-element.14.w_ref.w0_ref), channel_id=1, source_target_pairs={{0,1},{1,0},{2,3},{3,2},{4,5},{5,4},{6,7},{7,6},{8,9},{9,8},{10,11... | collective-permute-start | bytes 589832 | tf_op jit(solution)/shard_map/ppermute | solution.py:373
  7.9 0.1 pad.1.clone
  8.0 2.3 %to_grid.4.g0 = f32[288,256]{1,0:T(8,128)} custom-call(f32[384,128]{1,0:T(8,128)} %get-tuple-element.14.w_ref.w0_ref, bf16[96,192]{1,0:T(8,128)(2,1)} %constant.22.clone.table_ref, f32[48,128]{1,0:T(8,128)} %constant.24.clone.twr_ref, f32[48,128]{1,0:T(8,128)} %constant.25.clone.twi_ref, bf16[256,256]{1,0:T(8,128)(2,1)} %constant.26.clone.lh_ref, ...), custom_call_target="tpu_custom_call" | custom-call | flops 113246208 | bytes 900000 | tf_op jit(solution)/shard_map/to_grid/pallas_call | solution.py:137
  10.3 0.0 copy-done.4
  10.3 0.0 collective-permute-done.1.w_ref
  10.3 0.0 copy-start.2
  10.3 0.7 copy-done.2
  11.0 2.3 %to_grid.5.g1 = f32[288,256]{1,0:T(8,128)} custom-call(f32[384,128]{1,0:T(8,128)} %copy-done.2, bf16[96,192]{1,0:T(8,128)(2,1)} %constant.22.clone.table_ref, f32[48,128]{1,0:T(8,128)} %constant.24.clone.twr_ref, f32[48,128]{1,0:T(8,128)} %constant.25.clone.twi_ref, bf16[256,256]{1,0:T(8,128)(2,1)} %constant.26.clone.lh_ref, ...), custom_call_target="tpu_custom_call" | custom-call | flops 113246208 | bytes 900000 | tf_op jit(solution)/shard_map/to_grid/pallas_call | solution.py:137
  13.2 0.0 collective-permute-done.w_ref.w2_ref
  13.2 0.0 copy-start.1
  13.2 2.4 %collective-permute-start.2 = (f32[384,128]{1,0:T(8,128)S(1)}, f32[384,128]{1,0:T(8,128)S(1)}, u32[]{:S(2)}, u32[]{:S(2)}) collective-permute-start(f32[384,128]{1,0:T(8,128)S(1)} %collective-permute-done.w_ref.w2_ref), channel_id=1, source_target_pairs={{0,1},{1,0},{2,3},{3,2},{4,5},{5,4},{6,7},{7,6},{8,9},{9,8},{10,11... | collective-permute-start | bytes 589832 | tf_op jit(solution)/shard_map/ppermute | solution.py:373
  15.6 0.7 pad_maximum_fusion.mask_ref
  16.3 0.0 copy-done.1
  16.3 2.3 %to_grid.6.g2 = f32[288,256]{1,0:T(8,128)} custom-call(f32[384,128]{1,0:T(8,128)} %copy-done.1, bf16[96,192]{1,0:T(8,128)(2,1)} %constant.22.clone.table_ref, f32[48,128]{1,0:T(8,128)} %constant.24.clone.twr_ref, f32[48,128]{1,0:T(8,128)} %constant.25.clone.twi_ref, bf16[256,256]{1,0:T(8,128)(2,1)} %constant.26.clone.lh_ref, ...), custom_call_target="tpu_custom_call" | custom-call | flops 113246208 | bytes 900000 | tf_op jit(solution)/shard_map/to_grid/pallas_call | solution.py:137
  18.6 0.0 collective-permute-done.2.w_ref
  18.6 0.0 copy-start.3
  18.6 0.7 copy-done.3
  19.3 2.3 %to_grid.7.g3 = f32[288,256]{1,0:T(8,128)} custom-call(f32[384,128]{1,0:T(8,128)} %copy-done.3, bf16[96,192]{1,0:T(8,128)(2,1)} %constant.22.clone.table_ref, f32[48,128]{1,0:T(8,128)} %constant.24.clone.twr_ref, f32[48,128]{1,0:T(8,128)} %constant.25.clone.twi_ref, bf16[256,256]{1,0:T(8,128)(2,1)} %constant.26.clone.lh_ref, ...), custom_call_target="tpu_custom_call" | custom-call | flops 113246208 | bytes 900000 | tf_op jit(solution)/shard_map/to_grid/pallas_call | solution.py:137
  21.6 3.8 %to_rhs.1 = f32[768,128]{1,0:T(8,128)} custom-call(s32[1]{0:T(128)S(6)} %add.7.x_ref, f32[288,256]{1,0:T(8,128)} %to_grid.4.g0, f32[288,256]{1,0:T(8,128)} %to_grid.5.g1, f32[288,256]{1,0:T(8,128)} %to_grid.6.g2, f32[288,256]{1,0:T(8,128)} %to_grid.7.g3, f32[384,128]{1,0:T(8,128)} %get-tuple-element.14.w_ref.w0_ref, f32[384,128]{1,0:T(8,128)} %copy-done.1, ...), custom_call_target="tpu_custom_call" | custom-call | flops 226492416 | bytes 2400000 | tf_op jit(solution)/shard_map/to_rhs/pallas_call | solution.py:247
  25.3 23.2 %all-to-all-start = ((f32[256,1,384]{2,1,0:T(1,128)}), f32[256,1,384]{2,1,0:T(1,128)S(1)}, u32[]{:S(2)}, u32[]{:S(2)}) async-start(f32[256,1,384]{2,1,0:T(1,128)} %bitcast.12), calls=%async_computation | async-start | bytes 786432 | tf_op jit(solution)/shard_map/all_to_all | solution.py:369
  48.6 5.7 %solve_operator.1 = (bf16[768,768]{1,0:T(8,128)(2,1)}, bf16[768,768]{1,0:T(8,128)(2,1)}) custom-call(f32[6,128,128]{2,1,0:T(8,128)} %inv_ref.1, f32[5,128,128]{2,1,0:T(8,128)} %mult_ref.1), custom_call_target="tpu_custom_call" | custom-call | flops 2768240640 | bytes 3100000 | tf_op jit(solution)/shard_map/solve_operator/pallas_call | solution.py:313
  54.3 22.3 %all-to-all-done = f32[256,1,384]{2,1,0:T(1,128)S(1)} async-done(((f32[256,1,384]{2,1,0:T(1,128)}), f32[256,1,384]{2,1,0:T(1,128)S(1)}, u32[]{:S(2)}, u32[]{:S(2)}) %all-to-all-start) | async-done | bytes 393248 | tf_op jit(solution)/shard_map/all_to_all | solution.py:369
  76.6 0.0 copy-start
  76.6 0.8 copy-done
  77.3 3.9 %solve.1 = f32[768,128]{1,0:T(8,128)} custom-call(bf16[768,768]{1,0:T(8,128)(2,1)} %get-tuple-element.11.high_ref, bf16[768,768]{1,0:T(8,128)(2,1)} %get-tuple-element.12.low_ref, f32[768,128]{1,0:T(8,128)} %bitcast.13), custom_call_target="tpu_custom_call" | custom-call | tf_op jit(solution)/shard_map/solve/pallas_call | solution.py:339
  81.2 37.0 %all_to_all.10 = f32[128,1,768]{2,1,0:T(1,128)} all-to-all(f32[128,1,768]{2,1,0:T(1,128)} %bitcast.14), channel_id=1, replica_groups=mesh['wa'=128,'y'=2,'c'=2] {'wa'}, dimensions={0} | all-to-all | bytes 786432 | tf_op jit(solution)/shard_map/all_to_all | solution.py:369
  118.2 1.9 %spread.1 = (f32[360,128]{1,0:T(8,128)}, f32[360,128]{1,0:T(8,128)}) custom-call(f32[768,128]{1,0:T(8,128)} %bitcast.15), custom_call_target="tpu_custom_call" | custom-call | tf_op jit(solution)/shard_map/spread/pallas_call | solution.py:360
  (2 shorter events, 0.0 us)
Async XLA Ops:
  0.6 9.6 %copy-start.4 = (s32[3840]{0:T(1024)S(1)}, s32[3840]{0:T(1024)}, u32[]{:S(2)}) copy-start(s32[3840]{0:T(1024)} %param.13) | copy-start | bytes 46084
  2.5 10.8 %collective-permute-start = (f32[384,128]{1,0:T(8,128)}, f32[384,128]{1,0:T(8,128)S(1)}, u32[]{:S(2)}, u32[]{:S(2)}) collective-permute-start(f32[384,128]{1,0:T(8,128)} %get-tuple-element.13), channel_id=1, source_target_pairs={{0,2},{2,0},{1,3},{3,1},{4,6},{6,4},{5,7},{7,5},{8,10},{10,8},{9,1... | collective-permute-start | bytes 589832 | tf_op jit(solution)/shard_map/ppermute | solution.py:373
  5.9 4.3 %collective-permute-start.1 = (f32[384,128]{1,0:T(8,128)}, f32[384,128]{1,0:T(8,128)S(1)}, u32[]{:S(2)}, u32[]{:S(2)}) collective-permute-start(f32[384,128]{1,0:T(8,128)} %get-tuple-element.14.w_ref.w0_ref), channel_id=1, source_target_pairs={{0,1},{1,0},{2,3},{3,2},{4,5},{5,4},{6,7},{7,6},{8,9},{9,8},{10,11... | collective-permute-start | bytes 589832 | tf_op jit(solution)/shard_map/ppermute | solution.py:373
  10.3 0.7 copy-start.2
  13.2 3.1 %copy-start.1 = (f32[384,128]{1,0:T(8,128)}, f32[384,128]{1,0:T(8,128)S(1)}, u32[]{:S(2)}) copy-start(f32[384,128]{1,0:T(8,128)S(1)} %collective-permute-done.w_ref.w2_ref) | copy-start | bytes 589828
  13.2 5.4 %collective-permute-start.2 = (f32[384,128]{1,0:T(8,128)S(1)}, f32[384,128]{1,0:T(8,128)S(1)}, u32[]{:S(2)}, u32[]{:S(2)}) collective-permute-start(f32[384,128]{1,0:T(8,128)S(1)} %collective-permute-done.w_ref.w2_ref), channel_id=1, source_target_pairs={{0,1},{1,0},{2,3},{3,2},{4,5},{5,4},{6,7},{7,6},{8,9},{9,8},{10,11... | collective-permute-start | bytes 589832 | tf_op jit(solution)/shard_map/ppermute | solution.py:373
  18.6 0.7 copy-start.3
  25.3 51.2 %all-to-all-start = ((f32[256,1,384]{2,1,0:T(1,128)}), f32[256,1,384]{2,1,0:T(1,128)S(1)}, u32[]{:S(2)}, u32[]{:S(2)}) async-start(f32[256,1,384]{2,1,0:T(1,128)} %bitcast.12), calls=%async_computation | async-start | bytes 786432 | tf_op jit(solution)/shard_map/all_to_all | solution.py:369
  76.6 0.8 copy-start

commit v2 on v1

--- a/solution.py
+++ b/solution.py
@@ -20,6 +20,8 @@
 HALF = ROWS // 2
 SLOT = 48
 PADDED = 64
+JHALF = KEPT // 2
+GROUPS = 16
 PARTS = 2 * ROWS * KEPT
 
 
@@ -27,6 +29,14 @@
     high = table.astype(np.float32).astype(BF16)
     low = (table - high.astype(np.float64)).astype(np.float32).astype(BF16)
     return high, low
+
+
+def place(jhalf, part):
+    return 32 * jhalf + 16 * part + jhalf
+
+
+def flip_bits(z):
+    return int(f"{z:04b}"[::-1], 2)
 
 
 def build_tables():
@@ -39,16 +49,18 @@
     short = 2.0 * np.pi * ((n1[:, None] * kept[None, :]) % OUTER) / OUTER
     to_grid = np.zeros((2 * SLOT, 64))
     scale = 1.0 / math.sqrt(modes)
-    to_grid[:OUTER, 0:KEPT] = np.cos(short) * scale
-    to_grid[:OUTER, 34:64] = -np.sin(short) * scale
-    to_grid[SLOT : SLOT + OUTER, 0:KEPT] = np.sin(short) * scale
-    to_grid[SLOT : SLOT + OUTER, 34:64] = np.cos(short) * scale
+    re = np.array([place(j // half, 0) + j % half for j in range(KEPT)])
+    im = np.array([place(j // half, 1) + j % half for j in range(KEPT)])
+    to_grid[:OUTER, re] = np.cos(short) * scale
+    to_grid[:OUTER, im] = -np.sin(short) * scale
+    to_grid[SLOT : SLOT + OUTER, re] = np.sin(short) * scale
+    to_grid[SLOT : SLOT + OUTER, im] = np.cos(short) * scale
     to_modes = np.zeros((64, 2 * SLOT))
     scale = NL_COEFF / math.sqrt(length)
-    to_modes[0:KEPT, :OUTER] = np.cos(short).T * scale
-    to_modes[0:KEPT, SLOT : SLOT + OUTER] = -np.sin(short).T * scale
-    to_modes[34:64, :OUTER] = -np.sin(short).T * scale
-    to_modes[34:64, SLOT : SLOT + OUTER] = -np.cos(short).T * scale
+    to_modes[re, :OUTER] = np.cos(short).T * scale
+    to_modes[re, SLOT : SLOT + OUTER] = -np.sin(short).T * scale
+    to_modes[im, :OUTER] = -np.sin(short).T * scale
+    to_modes[im, SLOT : SLOT + OUTER] = -np.cos(short).T * scale
     twist = 2.0 * np.pi * (n1[:, None] * lane[None, :]) / length
     twist_re = np.zeros((SLOT, LANES), np.float32)
     twist_im = np.zeros((SLOT, LANES), np.float32)
@@ -70,6 +82,26 @@
     )
 
 
+def call(kernel, out_shapes, args, name, scratch=(), scalars=0, flops=0, out_space=pltpu.VMEM):
+    shapes = [jax.ShapeDtypeStruct(*shape) if out_space is None else out_space(*shape) for shape in out_shapes]
+    args = [
+        arg if i < scalars else pltpu.with_memory_space_constraint(arg, pltpu.VMEM)
+        for i, arg in enumerate(args)
+    ]
+    smem = pl.BlockSpec(memory_space=pltpu.SMEM)
+    vmem = pl.BlockSpec(memory_space=pltpu.VMEM)
+    return pl.pallas_call(
+        kernel,
+        out_shape=shapes,
+        in_specs=[smem] * scalars + [vmem] * (len(args) - scalars),
+        out_specs=[vmem] * len(shapes),
+        scratch_shapes=[pltpu.VMEM(*shape) for shape in scratch],
+        compiler_params=pltpu.CompilerParams(vmem_limit_bytes=16 << 20),
+        cost_estimate=pl.CostEstimate(flops=flops, bytes_accessed=1000000, transcendentals=0),
+        name=name,
+    )(*args)
+
+
 def dot(left, right):
     return jnp.dot(left, right, preferred_element_type=jnp.float32)
 
@@ -85,22 +117,17 @@
     for half, out_ref in ((1 - mine, send_ref), (mine, keep_ref)):
         for field, ref in enumerate((a_ref, b_ref)):
             for i in range(HALF):
-                base = half * (HALF * KEPT) + i * KEPT
                 row = (field * HALF + i) * PADDED
-                out_ref[pl.ds(row, 32), :] = ref[pl.ds(base, 32), :]
-                out_ref[pl.ds(row + 32, 32), :] = ref[pl.ds(base + PARTS // 2 - 2, 32), :]
+                for jhalf in range(2):
+                    for part in range(2):
+                        base = half * (HALF * KEPT) + part * (PARTS // 2) + i * KEPT
+                        base = base + jhalf * (JHALF - 1)
+                        out_ref[pl.ds(row + 32 * jhalf + 16 * part, 16), :] = ref[pl.ds(base, 16), :]
 
 
 def prepare(y, field_a, field_b):
-    vmem = pl.BlockSpec(memory_space=pltpu.VMEM)
-    shape = jax.ShapeDtypeStruct((2 * HALF * PADDED, LANES), jnp.float32)
-    return pl.pallas_call(
-        prepare_kernel,
-        out_shape=[shape, shape],
-        in_specs=[pl.BlockSpec(memory_space=pltpu.SMEM), vmem, vmem],
-        out_specs=[vmem, vmem],
-        name="prepare",
-    )(y, field_a, field_b)
+    shape = ((2 * HALF * PADDED, LANES), jnp.float32)
+    return call(prepare_kernel, [shape, shape], (y, field_a, field_b), "prepare", scalars=1)
 
 
 def load_modes(w_ref, field, i):
@@ -134,22 +161,16 @@
 
 def to_grid(own, tables):
     rows = 2 * HALF * SLOT
-    return pl.pallas_call(
+    names = ("to_grid", "twist_re", "twist_im", "lanes_h", "lanes_l")
+    (grid,) = call(
         grid_kernel,
-        out_shape=jax.ShapeDtypeStruct((rows, 2 * LANES), jnp.float32),
-        scratch_shapes=[pltpu.VMEM((rows, 2 * LANES), jnp.bfloat16)] * 2,
-        cost_estimate=pl.CostEstimate(
-            flops=2 * rows * 256 * 256 * 3, bytes_accessed=900000, transcendentals=0
-        ),
-        name="to_grid",
-    )(
-        own,
-        tables["to_grid"],
-        tables["twist_re"],
-        tables["twist_im"],
-        tables["lanes_h"],
-        tables["lanes_l"],
-    )
+        [((rows, 2 * LANES), jnp.float32)],
+        (own, *[tables[name] for name in names]),
+        "to_grid",
+        scratch=[((rows, 2 * LANES), jnp.bfloat16)] * 2,
+        flops=2 * rows * 256 * 256 * 12,
+    )
+    return grid
 
 
 def pairs_of(x, target):
@@ -161,8 +182,8 @@
 
 
 def modes_kernel(
-    x_ref, g0, g1, g2, g3, w0_ref, w2_ref, mask_ref, table_ref, twr_ref, twi_ref, lh_ref, ll_ref,
-    out_ref, uh_ref, ul_ref,
+    x_ref, g0, g1, g2, g3, w0_ref, w2_ref, keep_ref, table_ref, twr_ref, twi_ref, lh_ref, ll_ref,
+    out_ref, uh_ref, ul_ref, mask_ref,
 ):
     grids = (g0, g1, g2, g3)
     x = x_ref[0]
@@ -211,11 +232,17 @@
     spectra = lane_transform(uh_ref, ul_ref, lh_ref, ll_ref)
     table = table_ref[...]
     twr, twi = twr_ref[...], twi_ref[...]
+    mask_ref[...] = jnp.zeros_like(mask_ref)
+    for jhalf in range(2):
+        for part in range(2):
+            flags = keep_ref[pl.ds(jhalf * JHALF, JHALF), :].astype(jnp.float32)
+            mask_ref[pl.ds(place(jhalf, part), JHALF), :] = flags
     mask = mask_ref[...]
-    for row in range(ROWS):
+
+    def updated(target, i):
         re_parts, im_parts = [], []
         for field in range(2):
-            start = (2 * row + field) * SLOT
+            start = ((target * HALF + i) * 2 + field) * SLOT
             re = spectra[start : start + SLOT, :LANES]
             im = spectra[start : start + SLOT, LANES:]
             re_parts.append(re * twr - im * twi)
@@ -225,47 +252,35 @@
         )
         high, low = split(twisted)
         hat = dot(table, jnp.concatenate([high, low, high], axis=0))
-        mine = (x // 2) == row // HALF
-        columns = jnp.concatenate(
-            [
-                jnp.where(
-                    mine,
-                    load_modes(w0_ref, field, row % HALF),
-                    load_modes(w2_ref, field, row % HALF),
-                )
-                + hat[:, field * LANES : (field + 1) * LANES] * mask
-                for field in range(2)
-            ],
-            axis=0,
-        )
-        out_ref[pl.ds(row, LANES, stride=ROWS), :] = columns.T
-
-
-def to_rhs(x, grids, own, other, mask, tables):
+        mine = (x // 2) == target
+        return [
+            jnp.where(mine, load_modes(w0_ref, field, i), load_modes(w2_ref, field, i))
+            + hat[:, field * LANES : (field + 1) * LANES] * mask
+            for field in range(2)
+        ]
+
+    for i in range(HALF):
+        blocks = updated(0, i) + updated(1, i)
+        for jhalf in range(2):
+            columns = jnp.concatenate(
+                [block[32 * jhalf : 32 * jhalf + 32] for block in blocks], axis=0
+            )
+            out_ref[pl.ds(HALF * jhalf + i, LANES, stride=ROWS), :] = columns.T
+
+
+def to_rhs(x, grids, own, other, keep, tables):
     rows = 2 * ROWS * SLOT
-    vmem = pl.BlockSpec(memory_space=pltpu.VMEM)
-    return pl.pallas_call(
+    names = ("to_modes", "twist_re", "twist_im", "lanes_h", "lanes_l")
+    (rhs,) = call(
         modes_kernel,
-        out_shape=jax.ShapeDtypeStruct((ROWS * LANES, LANES), jnp.float32),
-        in_specs=[pl.BlockSpec(memory_space=pltpu.SMEM)] + [vmem] * 12,
-        out_specs=vmem,
-        scratch_shapes=[pltpu.VMEM((rows, 2 * LANES), jnp.bfloat16)] * 2,
-        cost_estimate=pl.CostEstimate(
-            flops=2 * rows * 256 * 256 * 3, bytes_accessed=2400000, transcendentals=0
-        ),
-        name="to_rhs",
-    )(
-        x,
-        *grids,
-        own,
-        other,
-        mask,
-        tables["to_modes"],
-        tables["twist_re"],
-        tables["twist_im"],
-        tables["lanes_h"],
-        tables["lanes_l"],
-    )
+        [((ROWS * LANES, LANES), jnp.float32)],
+        (x, *grids, own, other, keep, *[tables[name] for name in names]),
+        "to_rhs",
+        scratch=[((rows, 2 * LANES), jnp.bfloat16)] * 2 + [((PADDED, LANES), jnp.float32)],
+        scalars=1,
+        flops=2 * rows * 256 * 256 * 12,
+    )
+    return rhs
 
 
 def matmul3(left, right, contract=((1,), (0,))):
@@ -310,63 +325,75 @@
 
 def solve_operator(block_inv, lower_mult):
     size = block_inv.shape[0] * block_inv.shape[1]
-    return pl.pallas_call(
+    return call(
         operator_kernel,
-        out_shape=[jax.ShapeDtypeStruct((size, size), jnp.bfloat16)] * 2,
-        scratch_shapes=[pltpu.VMEM((size, size), jnp.float32)] * 2,
-        cost_estimate=pl.CostEstimate(
-            flops=2 * 55 * 3 * 128**3 * 4, bytes_accessed=3100000, transcendentals=0
-        ),
-        name="solve_operator",
-    )(block_inv, lower_mult)
-
-
-def solve_kernel(high_ref, low_ref, r_ref, out_ref, rh_ref):
-    @pl.when(pl.program_id(0) == 0)
-    def _():
-        high, low = split(r_ref[...])
-        rh_ref[:, :LANES] = high
-        rh_ref[:, LANES:] = low
-
+        [((size, size), jnp.bfloat16)] * 2,
+        (block_inv, lower_mult),
+        "solve_operator",
+        scratch=[((size, size), jnp.float32)] * 2,
+        flops=2 * 55 * 3 * 128**3 * 4,
+    )
+
+
+def solve_kernel(high_ref, low_ref, r_ref, out_ref, rh_ref, n_ref):
+    size = r_ref.shape[0]
+    group = size // GROUPS
+    for z in range(GROUPS):
+        high, low = split(r_ref[pl.ds(flip_bits(z) * group, group), :])
+        rh_ref[pl.ds(z * group, group), :LANES] = high
+        rh_ref[pl.ds(z * group, group), LANES:] = low
     both = dot(high_ref[...], rh_ref[...])
-    out_ref[...] = both[:, :LANES] + both[:, LANES:] + dot(low_ref[...], rh_ref[:, :LANES])
+    solved = both[:, :LANES] + both[:, LANES:] + dot(low_ref[...], rh_ref[:, :LANES])
+    for z in range(GROUPS):
+        n_ref[pl.ds(flip_bits(z) * group, group), :] = solved[z * group : (z + 1) * group]
+    for i in range(HALF):
+        first = n_ref[pl.ds(i, LANES, stride=ROWS), :]
+        second = n_ref[pl.ds(HALF + i, LANES, stride=ROWS), :]
+        for target in range(2):
+            lanes = slice(target * 64, target * 64 + 64)
+            out_ref[pl.ds(HALF * target + i, LANES, stride=ROWS), :] = jnp.concatenate(
+                [first[:, lanes], second[:, lanes]], axis=1
+            )
 
 
 def solve(operator, rhs):
     size = rhs.shape[0]
-    steps = 3
-    blocks = pl.BlockSpec((size // steps, size), lambda i: (i, 0))
-    return pl.pallas_call(
+    (solved,) = call(
         solve_kernel,
-        out_shape=jax.ShapeDtypeStruct(rhs.shape, jnp.float32),
-        grid=(steps,),
-        in_specs=[blocks, blocks, pl.BlockSpec((size, LANES), lambda i: (0, 0))],
-        out_specs=pl.BlockSpec((size // steps, LANES), lambda i: (i, 0)),
-        scratch_shapes=[pltpu.VMEM((size, 2 * LANES), jnp.bfloat16)],
-        name="solve",
-    )(*operator, rhs)
+        [(rhs.shape, jnp.float32)],
+        (*operator, rhs),
+        "solve",
+        scratch=[((size, 2 * LANES), jnp.bfloat16), (rhs.shape, jnp.float32)],
+        flops=2 * size * size * 256 * 2,
+    )
+    return solved
 
 
 def spread_kernel(s_ref, a_ref, b_ref):
-    for row in range(ROWS):
-        columns = s_ref[pl.ds(row, LANES, stride=ROWS), :].T
-        for field, ref in enumerate((a_ref, b_ref)):
-            base = field * 64
-            ref[pl.ds(row * KEPT, KEPT), :] = columns[base : base + KEPT]
-            ref[pl.ds(PARTS // 2 + row * KEPT, KEPT), :] = columns[base + 34 : base + 64]
+    for jhalf in range(2):
+        for i in range(HALF):
+            columns = s_ref[pl.ds(HALF * jhalf + i, LANES, stride=ROWS), :].T
+            for second in range(2):
+                for field, ref in enumerate((a_ref, b_ref)):
+                    for part in range(2):
+                        start = second * 64 + field * 32 + part * 16 + jhalf
+                        row = part * (PARTS // 2) + (i + HALF * second) * KEPT + jhalf * JHALF
+                        ref[pl.ds(row, JHALF), :] = columns[start : start + JHALF]
 
 
 def spread(solved):
-    return pl.pallas_call(
-        spread_kernel,
-        out_shape=[jax.ShapeDtypeStruct((PARTS, LANES), jnp.float32)] * 2,
-        name="spread",
-    )(solved)
-
-
-def exchange(rows, axes, count):
-    sent = rows.reshape(count, 1, ROWS * LANES * LANES // count)
-    return lax.all_to_all(sent, axes, 0, 0, tiled=True).reshape(rows.shape)
+    return call(
+        spread_kernel, [((PARTS, LANES), jnp.float32)] * 2, (solved,), "spread", out_space=None
+    )
+
+
+ORDER = ("z0", "z1", "z2", "z3", "r", "y")
+
+
+def exchange(rows):
+    count = 2 * LANES
+    sent = rows.reshape(count, 1, rows.size // count)
+    return lax.all_to_all(sent, ORDER, 0, 0, tiled=True).reshape(rows.shape)
 
 
 def swap(value, axis):
@@ -384,21 +411,16 @@
     two, *grids = lax.optimization_barrier((two, *grids))
     three = swap(two, "c")
     grids += [to_grid(two, tables), to_grid(three, tables)]
-
-    keep = keep_mask.astype(jnp.float32).reshape(KEPT, LANES)
-    gap = jnp.zeros((2, LANES), jnp.float32)
-    mask = jnp.concatenate([keep, gap, gap, keep], axis=0)
-    rhs = to_rhs(x, grids, own, two, mask, tables)
+    rhs = to_rhs(x, grids, own, two, keep_mask.reshape(KEPT, LANES), tables)
     operator = solve_operator(block_inv, lower_mult)
-    solved = solve(operator, exchange(rhs, ("wa", "y"), 256))
-    new_a, new_b = spread(exchange(solved, "wa", 128))
+    new_a, new_b = spread(exchange(solve(operator, exchange(rhs))))
     return (new_a.reshape(field_a.shape), new_b.reshape(field_b.shape))
 
 
 def solution(mesh):
-    wa, gx = mesh.devices.shape
-    fine = Mesh(mesh.devices.reshape(wa, 2, gx // 2), ("wa", "y", "c"))
-    fields = P(None, ("y", "c"), "wa", None)
+    names = ("z3", "z2", "z1", "z0", "r", "y", "c")
+    fine = Mesh(mesh.devices.reshape(2, 2, 2, 2, 8, 2, 2), names)
+    fields = P(None, ("y", "c"), names[:5], None)
     return jax.shard_map(
         body,
         mesh=fine,

time: 121 us -> 110 us (0.909)
  Pallas kernels: 26.2 us -> 9.25 us
  local copies, waits for them, and re-layouts: 2.2 us -> 5.97 us
  waiting for transfers between devices: 22.3 us -> 25 us
    pallas_call x9, Pallas kernels: 26.2 us -> 9.25 us  [call(): pl.pallas_call(kernel, out_shape=shapes, in_specs=[smem] * scalars + [vme...]
    unnamed x10 -> x32, local copies, waits for them, and re-layouts: 2.12 us -> 5.97 us
    ppermute x3, waiting for transfers between devices: 0.01 us -> 1.49 us  [swap(): return lax.ppermute(value, axis, [(0, 1), (1, 0)])]
    all_to_all x1, waiting for transfers between devices: 22.3 us -> 23.5 us  [exchange(): return lax.all_to_all(sent, ORDER, 0, 0, tiled=True).reshape(rows.shape)]
  transfers between devices with their start and end apart: 4 -> 4, of which waited for: 1 -> 3; matrix products, arithmetic and copies ran while one was open for 1% -> 0% of each run, Pallas kernels for 10% -> 4%
where the time goes in v2:
time: 110 us; the launch traced here: 108 us
  blocking collectives  36.3 us (33%)
  starting transfers between devices  30.8 us (28%)
  waiting for transfers between devices  25 us (23%)
  Pallas kernels  9.25 us (8%)
  local copies, waits for them, and re-layouts  5.97 us (5%)
    all_to_all x1, blocking collectives, exchange(): return lax.all_to_all(sent, ORDER, 0, 0, tiled=True).reshape(rows.shape)  36.3 us
    all_to_all x1, waiting for transfers between devices, exchange(): return lax.all_to_all(sent, ORDER, 0, 0, tiled=True).reshape(rows.shape)  23.5 us
    all_to_all x1, starting transfers between devices, exchange(): return lax.all_to_all(sent, ORDER, 0, 0, tiled=True).reshape(rows.shape)  23.5 us
    pallas_call x9, Pallas kernels, call(): pl.pallas_call(kernel, out_shape=shapes, in_specs=[smem] * scalars + [vme...  9.25 us
    ppermute x3, starting transfers between devices, swap(): return lax.ppermute(value, axis, [(0, 1), (1, 0)])  7.31 us
    unnamed x32, local copies, waits for them, and re-layouts  5.97 us
  transfers between devices with their start and end apart: 4, of which 3 were waited for; matrix products, arithmetic and copies ran while one was open for 0% of the time, Pallas kernels for 4%

profile of v2, /device:TPU:6, one launch (start us, length us, event | category | flops | bytes accessed | tf_op | source)
XLA Modules:
  0.0 108.2 jit_solution(1185066147517196637)
XLA Ops:
  0.6 0.9 copy-done
  1.6 0.9 copy-done.1
  2.5 1.9 %collective-permute-start.1 = (f32[384,128]{1,0:T(8,128)S(1)}, f32[384,128]{1,0:T(8,128)S(1)}, u32[]{:S(2)}, u32[]{:S(2)}) collective-permute-start(f32[384,128]{1,0:T(8,128)S(1)} %get-tuple-element.14.w_ref.w0_ref), channel_id=1, source_target_pairs={{0,1},{1,0},{2,3},{3,2},{4,5},{5,4},{6,7},{7,6},{8,9},{9,8},{10,11... | collective-permute-start | bytes 589832 | tf_op jit(solution)/shard_map/ppermute | solution.py:400
  4.4 3.5 %collective-permute-start = (f32[384,128]{1,0:T(8,128)S(1)}, f32[384,128]{1,0:T(8,128)S(1)}, u32[]{:S(2)}, u32[]{:S(2)}) collective-permute-start(f32[384,128]{1,0:T(8,128)S(1)} %get-tuple-element.13), channel_id=1, source_target_pairs={{0,2},{2,0},{1,3},{3,1},{4,6},{6,4},{5,7},{7,5},{8,10},{10,8},{9,1... | collective-permute-start | bytes 589832 | tf_op jit(solution)/shard_map/ppermute | solution.py:400
  7.9 0.0 copy-start.5
  7.9 0.9 copy-done.5
  8.8 0.9 copy-done.7
  9.7 0.8 copy-done.10
  10.5 0.7 copy-done.12
  11.3 0.7 copy-done.14
  12.0 0.5 to_grid.4.g0
  12.5 0.0 copy-start.6
  12.5 0.0 copy-start.8
  12.5 0.0 copy-start.11
  12.5 0.0 copy-start.13
  12.5 0.0 copy-start.15
  12.6 0.5 to_grid.5.g1
  13.0 0.6 collective-permute-done.w_ref.w2_ref
  13.6 1.9 %collective-permute-start.2 = (f32[384,128]{1,0:T(8,128)S(1)}, f32[384,128]{1,0:T(8,128)S(1)}, u32[]{:S(2)}, u32[]{:S(2)}) collective-permute-start(f32[384,128]{1,0:T(8,128)S(1)} %collective-permute-done.w_ref.w2_ref), channel_id=1, source_target_pairs={{0,1},{1,0},{2,3},{3,2},{4,5},{5,4},{6,7},{7,6},{8,9},{9,8},{10,11... | collective-permute-start | bytes 589832 | tf_op jit(solution)/shard_map/ppermute | solution.py:400
  15.6 0.5 to_grid.6.g2
  16.1 0.0 copy-start.4
  16.1 0.0 copy-start.9
  16.1 0.9 collective-permute-done.2.w_ref
  17.0 0.5 to_grid.7.g3
  17.5 0.0 copy-start.3
  17.5 2.3 %to_rhs.1 = f32[768,128]{1,0:T(8,128)} custom-call(s32[1]{0:T(128)S(6)} %add.7.x_ref, f32[288,256]{1,0:T(8,128)S(1)} %to_grid.4.g0, f32[288,256]{1,0:T(8,128)S(1)} %to_grid.5.g1, f32[288,256]{1,0:T(8,128)S(1)} %to_grid.6.g2, f32[288,256]{1,0:T(8,128)S(1)} %to_grid.7.g3, f32[384,128]{1,0:T(8,128)S(1)} %get-tuple-element.14.w_ref.w0_ref, ...), custom_call_target="tpu_custom_call" | custom-call | flops 905969664 | bytes 1000000 | tf_op jit(solution)/shard_map/to_rhs/pallas_call | solution.py:93
  19.8 23.5 %all-to-all-start = ((f32[256,1,384]{2,1,0:T(1,128)}), f32[256,1,384]{2,1,0:T(1,128)S(1)}, u32[]{:S(2)}, u32[]{:S(2)}) async-start(f32[256,1,384]{2,1,0:T(1,128)} %bitcast.5), calls=%async_computation | async-start | bytes 786432 | tf_op jit(solution)/shard_map/all_to_all | solution.py:396
  43.3 3.2 %solve_operator.1 = (bf16[768,768]{1,0:T(8,128)(2,1)S(1)}, bf16[768,768]{1,0:T(8,128)(2,1)S(1)}) custom-call(f32[6,128,128]{2,1,0:T(8,128)S(1)} %copy-done.2, f32[5,128,128]{2,1,0:T(8,128)S(1)} %copy-done.3), custom_call_target="tpu_custom_call" | custom-call | flops 2768240640 | bytes 1000000 | tf_op jit(solution)/shard_map/solve_operator/pallas_call | solution.py:93
  46.6 23.5 %all-to-all-done = f32[256,1,384]{2,1,0:T(1,128)S(1)} async-done(((f32[256,1,384]{2,1,0:T(1,128)}), f32[256,1,384]{2,1,0:T(1,128)S(1)}, u32[]{:S(2)}, u32[]{:S(2)}) %all-to-all-start) | async-done | bytes 393248 | tf_op jit(solution)/shard_map/all_to_all | solution.py:396
  70.1 1.0 solve.1
  71.1 36.3 %all_to_all.10 = f32[256,1,384]{2,1,0:T(1,128)S(1)} all-to-all(f32[256,1,384]{2,1,0:T(1,128)S(1)} %bitcast.12), channel_id=1, replica_groups=mesh['z3'=2,'z2'=2,'z1'=2,'z0'=2,'r'=8,'y'=2,'c'=2] {'z0','z1','z2','z3'..., dimensions={0} | all-to-all | bytes 786432 | tf_op jit(solution)/shard_map/all_to_all | solution.py:396
  107.3 0.9 spread.1
  (18 shorter events, 0.1 us)
Async XLA Ops:
  0.6 0.9 copy-start
  1.6 0.9 copy-start.1
  2.5 10.0 %collective-permute-start.1 = (f32[384,128]{1,0:T(8,128)S(1)}, f32[384,128]{1,0:T(8,128)S(1)}, u32[]{:S(2)}, u32[]{:S(2)}) collective-permute-start(f32[384,128]{1,0:T(8,128)S(1)} %get-tuple-element.14.w_ref.w0_ref), channel_id=1, source_target_pairs={{0,1},{1,0},{2,3},{3,2},{4,5},{5,4},{6,7},{7,6},{8,9},{9,8},{10,11... | collective-permute-start | bytes 589832 | tf_op jit(solution)/shard_map/ppermute | solution.py:400
  4.4 9.2 %collective-permute-start = (f32[384,128]{1,0:T(8,128)S(1)}, f32[384,128]{1,0:T(8,128)S(1)}, u32[]{:S(2)}, u32[]{:S(2)}) collective-permute-start(f32[384,128]{1,0:T(8,128)S(1)} %get-tuple-element.13), channel_id=1, source_target_pairs={{0,2},{2,0},{1,3},{3,1},{4,6},{6,4},{5,7},{7,5},{8,10},{10,8},{9,1... | collective-permute-start | bytes 589832 | tf_op jit(solution)/shard_map/ppermute | solution.py:400
  7.9 0.9 copy-start.5
  8.8 0.9 copy-start.7
  9.7 0.8 copy-start.10
  10.5 0.7 copy-start.12
  11.3 0.7 copy-start.14
  12.5 3.1 %copy-start.6 = (bf16[256,256]{1,0:T(8,128)(2,1)S(1)}, bf16[256,256]{1,0:T(8,128)(2,1)}, u32[]{:S(2)}) copy-start(bf16[256,256]{1,0:T(8,128)(2,1)} %constant.25.clone.ll_ref) | copy-start | bytes 393220
  12.5 3.1 %copy-start.8 = (bf16[256,256]{1,0:T(8,128)(2,1)S(1)}, bf16[256,256]{1,0:T(8,128)(2,1)}, u32[]{:S(2)}) copy-start(bf16[256,256]{1,0:T(8,128)(2,1)} %constant.24.clone.lh_ref) | copy-start | bytes 393220
  12.5 3.1 %copy-start.11 = (bf16[96,192]{1,0:T(8,128)(2,1)S(1)}, bf16[96,192]{1,0:T(8,128)(2,1)}, u32[]{:S(2)}) copy-start(bf16[96,192]{1,0:T(8,128)(2,1)} %constant.20.clone.table_ref) | copy-start | bytes 110596
  12.5 3.1 %copy-start.13 = (f32[48,128]{1,0:T(8,128)S(1)}, f32[48,128]{1,0:T(8,128)}, u32[]{:S(2)}) copy-start(f32[48,128]{1,0:T(8,128)} %constant.23.clone.twi_ref) | copy-start | bytes 73732
  12.5 3.1 %copy-start.15 = (f32[48,128]{1,0:T(8,128)S(1)}, f32[48,128]{1,0:T(8,128)}, u32[]{:S(2)}) copy-start(f32[48,128]{1,0:T(8,128)} %constant.22.clone.twr_ref) | copy-start | bytes 73732
  13.6 3.3 %collective-permute-start.2 = (f32[384,128]{1,0:T(8,128)S(1)}, f32[384,128]{1,0:T(8,128)S(1)}, u32[]{:S(2)}, u32[]{:S(2)}) collective-permute-start(f32[384,128]{1,0:T(8,128)S(1)} %collective-permute-done.w_ref.w2_ref), channel_id=1, source_target_pairs={{0,1},{1,0},{2,3},{3,2},{4,5},{5,4},{6,7},{7,6},{8,9},{9,8},{10,11... | collective-permute-start | bytes 589832 | tf_op jit(solution)/shard_map/ppermute | solution.py:400
  16.1 1.3 %copy-start.4 = (s32[3840]{0:T(1024)S(1)}, s32[3840]{0:T(1024)}, u32[]{:S(2)}) copy-start(s32[3840]{0:T(1024)} %param.13) | copy-start | bytes 46084
  16.1 1.3 %copy-start.9 = (bf16[64,288]{1,0:T(8,128)(2,1)S(1)}, bf16[64,288]{1,0:T(8,128)(2,1)}, u32[]{:S(2)}) copy-start(bf16[64,288]{1,0:T(8,128)(2,1)} %constant.21.clone.table_ref) | copy-start | bytes 110596
  17.4 25.9 %copy-start.2 = (f32[6,128,128]{2,1,0:T(8,128)S(1)}, f32[6,128,128]{2,1,0:T(8,128)}, u32[]{:S(2)}) copy-start(f32[6,128,128]{2,1,0:T(8,128)} %inv_ref.1) | copy-start | bytes 1179652
  17.5 25.9 %copy-start.3 = (f32[5,128,128]{2,1,0:T(8,128)S(1)}, f32[5,128,128]{2,1,0:T(8,128)}, u32[]{:S(2)}) copy-start(f32[5,128,128]{2,1,0:T(8,128)} %mult_ref.1) | copy-start | bytes 983044
  19.8 50.3 %all-to-all-start = ((f32[256,1,384]{2,1,0:T(1,128)}), f32[256,1,384]{2,1,0:T(1,128)S(1)}, u32[]{:S(2)}, u32[]{:S(2)}) async-start(f32[256,1,384]{2,1,0:T(1,128)} %bitcast.5), calls=%async_computation | async-start | bytes 786432 | tf_op jit(solution)/shard_map/all_to_all | solution.py:396

commit v3 on v2

--- a/solution.py
+++ b/solution.py
@@ -21,7 +21,6 @@
 SLOT = 48
 PADDED = 64
 JHALF = KEPT // 2
-GROUPS = 16
 PARTS = 2 * ROWS * KEPT
 
 
@@ -33,10 +32,6 @@
 
 def place(jhalf, part):
     return 32 * jhalf + 16 * part + jhalf
-
-
-def flip_bits(z):
-    return int(f"{z:04b}"[::-1], 2)
 
 
 def build_tables():
@@ -335,17 +330,10 @@
     )
 
 
-def solve_kernel(high_ref, low_ref, r_ref, out_ref, rh_ref, n_ref):
-    size = r_ref.shape[0]
-    group = size // GROUPS
-    for z in range(GROUPS):
-        high, low = split(r_ref[pl.ds(flip_bits(z) * group, group), :])
-        rh_ref[pl.ds(z * group, group), :LANES] = high
-        rh_ref[pl.ds(z * group, group), LANES:] = low
-    both = dot(high_ref[...], rh_ref[...])
-    solved = both[:, :LANES] + both[:, LANES:] + dot(low_ref[...], rh_ref[:, :LANES])
-    for z in range(GROUPS):
-        n_ref[pl.ds(flip_bits(z) * group, group), :] = solved[z * group : (z + 1) * group]
+def solve_kernel(high_ref, low_ref, r_ref, out_ref, n_ref):
+    high, low = split(r_ref[...])
+    both = dot(high_ref[...], jnp.concatenate([high, low], axis=1))
+    n_ref[...] = both[:, :LANES] + both[:, LANES:] + dot(low_ref[...], high)
     for i in range(HALF):
         first = n_ref[pl.ds(i, LANES, stride=ROWS), :]
         second = n_ref[pl.ds(HALF + i, LANES, stride=ROWS), :]
@@ -363,7 +351,7 @@
         [(rhs.shape, jnp.float32)],
         (*operator, rhs),
         "solve",
-        scratch=[((size, 2 * LANES), jnp.bfloat16), (rhs.shape, jnp.float32)],
+        scratch=[(rhs.shape, jnp.float32)],
         flops=2 * size * size * 256 * 2,
     )
     return solved
@@ -387,7 +375,7 @@
     )
 
 
-ORDER = ("z0", "z1", "z2", "z3", "r", "y")
+ORDER = ("wa", "y")
 
 
 def exchange(rows):
@@ -418,9 +406,9 @@
 
 
 def solution(mesh):
-    names = ("z3", "z2", "z1", "z0", "r", "y", "c")
-    fine = Mesh(mesh.devices.reshape(2, 2, 2, 2, 8, 2, 2), names)
-    fields = P(None, ("y", "c"), names[:5], None)
+    wa, gx = mesh.devices.shape
+    fine = Mesh(mesh.devices.reshape(wa, 2, gx // 2), ("wa", "y", "c"))
+    fields = P(None, ("y", "c"), "wa", None)
     return jax.shard_map(
         body,
         mesh=fine,

time: 110 us -> 112 us (1.018)
  waiting for transfers between devices: 25 us -> 26.4 us
    all_to_all x1, waiting for transfers between devices: 23.5 us -> 24.9 us  [exchange(): return lax.all_to_all(sent, ORDER, 0, 0, tiled=True).reshape(rows.shape)]
where the time goes in v3:
time: 112 us; the launch traced here: 110 us
  blocking collectives  36.9 us (33%)
  starting transfers between devices  30.8 us (28%)
  waiting for transfers between devices  26.4 us (24%)
  Pallas kernels  9.18 us (8%)
  local copies, waits for them, and re-layouts  5.97 us (5%)
    all_to_all x1, blocking collectives, exchange(): return lax.all_to_all(sent, ORDER, 0, 0, tiled=True).reshape(rows.shape)  36.9 us
    all_to_all x1, waiting for transfers between devices, exchange(): return lax.all_to_all(sent, ORDER, 0, 0, tiled=True).reshape(rows.shape)  24.9 us
    all_to_all x1, starting transfers between devices, exchange(): return lax.all_to_all(sent, ORDER, 0, 0, tiled=True).reshape(rows.shape)  23.5 us
    pallas_call x9, Pallas kernels, call(): pl.pallas_call(kernel, out_shape=shapes, in_specs=[smem] * scalars + [vme...  9.18 us
    ppermute x3, starting transfers between devices, swap(): return lax.ppermute(value, axis, [(0, 1), (1, 0)])  7.31 us
    unnamed x32, local copies, waits for them, and re-layouts  5.97 us
  transfers between devices with their start and end apart: 4, of which 3 were waited for; matrix products, arithmetic and copies ran while one was open for 0% of the time, Pallas kernels for 4%

profile of v3, /device:TPU:6, one launch (start us, length us, event | category | flops | bytes accessed | tf_op | source)
XLA Modules:
  0.0 110.2 jit_solution(11112924259563067096)
XLA Ops:
  0.6 0.9 copy-done
  1.6 0.9 copy-done.1
  2.5 1.9 %collective-permute-start.1 = (f32[384,128]{1,0:T(8,128)S(1)}, f32[384,128]{1,0:T(8,128)S(1)}, u32[]{:S(2)}, u32[]{:S(2)}) collective-permute-start(f32[384,128]{1,0:T(8,128)S(1)} %get-tuple-element.14.w_ref.w0_ref), channel_id=1, source_target_pairs={{0,1},{1,0},{2,3},{3,2},{4,5},{5,4},{6,7},{7,6},{8,9},{9,8},{10,11... | collective-permute-start | bytes 589832 | tf_op jit(solution)/shard_map/ppermute | solution.py:388
  4.4 3.5 %collective-permute-start = (f32[384,128]{1,0:T(8,128)S(1)}, f32[384,128]{1,0:T(8,128)S(1)}, u32[]{:S(2)}, u32[]{:S(2)}) collective-permute-start(f32[384,128]{1,0:T(8,128)S(1)} %get-tuple-element.13), channel_id=1, source_target_pairs={{0,2},{2,0},{1,3},{3,1},{4,6},{6,4},{5,7},{7,5},{8,10},{10,8},{9,1... | collective-permute-start | bytes 589832 | tf_op jit(solution)/shard_map/ppermute | solution.py:388
  7.9 0.0 copy-start.5
  7.9 0.9 copy-done.5
  8.8 0.9 copy-done.7
  9.7 0.8 copy-done.10
  10.5 0.7 copy-done.12
  11.3 0.7 copy-done.14
  12.0 0.5 to_grid.4.g0
  12.5 0.0 copy-start.6
  12.5 0.0 copy-start.8
  12.5 0.0 copy-start.11
  12.5 0.0 copy-start.13
  12.5 0.0 copy-start.15
  12.6 0.5 to_grid.5.g1
  13.0 0.6 collective-permute-done.w_ref.w2_ref
  13.6 1.9 %collective-permute-start.2 = (f32[384,128]{1,0:T(8,128)S(1)}, f32[384,128]{1,0:T(8,128)S(1)}, u32[]{:S(2)}, u32[]{:S(2)}) collective-permute-start(f32[384,128]{1,0:T(8,128)S(1)} %collective-permute-done.w_ref.w2_ref), channel_id=1, source_target_pairs={{0,1},{1,0},{2,3},{3,2},{4,5},{5,4},{6,7},{7,6},{8,9},{9,8},{10,11... | collective-permute-start | bytes 589832 | tf_op jit(solution)/shard_map/ppermute | solution.py:388
  15.6 0.5 to_grid.6.g2
  16.1 0.0 copy-start.4
  16.1 0.0 copy-start.9
  16.1 0.9 collective-permute-done.2.w_ref
  17.0 0.5 to_grid.7.g3
  17.5 0.0 copy-start.3
  17.5 2.3 %to_rhs.1 = f32[768,128]{1,0:T(8,128)} custom-call(s32[1]{0:T(128)S(6)} %add.7.x_ref, f32[288,256]{1,0:T(8,128)S(1)} %to_grid.4.g0, f32[288,256]{1,0:T(8,128)S(1)} %to_grid.5.g1, f32[288,256]{1,0:T(8,128)S(1)} %to_grid.6.g2, f32[288,256]{1,0:T(8,128)S(1)} %to_grid.7.g3, f32[384,128]{1,0:T(8,128)S(1)} %get-tuple-element.14.w_ref.w0_ref, ...), custom_call_target="tpu_custom_call" | custom-call | flops 905969664 | bytes 1000000 | tf_op jit(solution)/shard_map/to_rhs/pallas_call | solution.py:88
  19.8 23.5 %all-to-all-start = ((f32[256,1,384]{2,1,0:T(1,128)}), f32[256,1,384]{2,1,0:T(1,128)S(1)}, u32[]{:S(2)}, u32[]{:S(2)}) async-start(f32[256,1,384]{2,1,0:T(1,128)} %bitcast.5), calls=%async_computation | async-start | bytes 786432 | tf_op jit(solution)/shard_map/all_to_all | solution.py:384
  43.3 3.2 %solve_operator.1 = (bf16[768,768]{1,0:T(8,128)(2,1)S(1)}, bf16[768,768]{1,0:T(8,128)(2,1)S(1)}) custom-call(f32[6,128,128]{2,1,0:T(8,128)S(1)} %copy-done.2, f32[5,128,128]{2,1,0:T(8,128)S(1)} %copy-done.3), custom_call_target="tpu_custom_call" | custom-call | flops 2768240640 | bytes 1000000 | tf_op jit(solution)/shard_map/solve_operator/pallas_call | solution.py:88
  46.6 24.9 %all-to-all-done = f32[256,1,384]{2,1,0:T(1,128)S(1)} async-done(((f32[256,1,384]{2,1,0:T(1,128)}), f32[256,1,384]{2,1,0:T(1,128)S(1)}, u32[]{:S(2)}, u32[]{:S(2)}) %all-to-all-start) | async-done | bytes 393248 | tf_op jit(solution)/shard_map/all_to_all | solution.py:384
  71.5 0.9 solve.1
  72.4 36.9 %all_to_all.10 = f32[256,1,384]{2,1,0:T(1,128)S(1)} all-to-all(f32[256,1,384]{2,1,0:T(1,128)S(1)} %bitcast.12), channel_id=1, replica_groups=mesh['wa'=128,'y'=2,'c'=2] {'wa','y'}, dimensions={0} | all-to-all | bytes 786432 | tf_op jit(solution)/shard_map/all_to_all | solution.py:384
  109.3 0.9 spread.1
  (18 shorter events, 0.1 us)
Async XLA Ops:
  0.6 0.9 copy-start
  1.6 0.9 copy-start.1
  2.5 10.0 %collective-permute-start.1 = (f32[384,128]{1,0:T(8,128)S(1)}, f32[384,128]{1,0:T(8,128)S(1)}, u32[]{:S(2)}, u32[]{:S(2)}) collective-permute-start(f32[384,128]{1,0:T(8,128)S(1)} %get-tuple-element.14.w_ref.w0_ref), channel_id=1, source_target_pairs={{0,1},{1,0},{2,3},{3,2},{4,5},{5,4},{6,7},{7,6},{8,9},{9,8},{10,11... | collective-permute-start | bytes 589832 | tf_op jit(solution)/shard_map/ppermute | solution.py:388
  4.4 9.2 %collective-permute-start = (f32[384,128]{1,0:T(8,128)S(1)}, f32[384,128]{1,0:T(8,128)S(1)}, u32[]{:S(2)}, u32[]{:S(2)}) collective-permute-start(f32[384,128]{1,0:T(8,128)S(1)} %get-tuple-element.13), channel_id=1, source_target_pairs={{0,2},{2,0},{1,3},{3,1},{4,6},{6,4},{5,7},{7,5},{8,10},{10,8},{9,1... | collective-permute-start | bytes 589832 | tf_op jit(solution)/shard_map/ppermute | solution.py:388
  7.9 0.9 copy-start.5
  8.8 0.9 copy-start.7
  9.7 0.8 copy-start.10
  10.5 0.7 copy-start.12
  11.3 0.7 copy-start.14
  12.5 3.1 %copy-start.6 = (bf16[256,256]{1,0:T(8,128)(2,1)S(1)}, bf16[256,256]{1,0:T(8,128)(2,1)}, u32[]{:S(2)}) copy-start(bf16[256,256]{1,0:T(8,128)(2,1)} %constant.25.clone.ll_ref) | copy-start | bytes 393220
  12.5 3.1 %copy-start.8 = (bf16[256,256]{1,0:T(8,128)(2,1)S(1)}, bf16[256,256]{1,0:T(8,128)(2,1)}, u32[]{:S(2)}) copy-start(bf16[256,256]{1,0:T(8,128)(2,1)} %constant.24.clone.lh_ref) | copy-start | bytes 393220
  12.5 3.1 %copy-start.11 = (bf16[96,192]{1,0:T(8,128)(2,1)S(1)}, bf16[96,192]{1,0:T(8,128)(2,1)}, u32[]{:S(2)}) copy-start(bf16[96,192]{1,0:T(8,128)(2,1)} %constant.20.clone.table_ref) | copy-start | bytes 110596
  12.5 3.1 %copy-start.13 = (f32[48,128]{1,0:T(8,128)S(1)}, f32[48,128]{1,0:T(8,128)}, u32[]{:S(2)}) copy-start(f32[48,128]{1,0:T(8,128)} %constant.23.clone.twi_ref) | copy-start | bytes 73732
  12.5 3.1 %copy-start.15 = (f32[48,128]{1,0:T(8,128)S(1)}, f32[48,128]{1,0:T(8,128)}, u32[]{:S(2)}) copy-start(f32[48,128]{1,0:T(8,128)} %constant.22.clone.twr_ref) | copy-start | bytes 73732
  13.6 3.3 %collective-permute-start.2 = (f32[384,128]{1,0:T(8,128)S(1)}, f32[384,128]{1,0:T(8,128)S(1)}, u32[]{:S(2)}, u32[]{:S(2)}) collective-permute-start(f32[384,128]{1,0:T(8,128)S(1)} %collective-permute-done.w_ref.w2_ref), channel_id=1, source_target_pairs={{0,1},{1,0},{2,3},{3,2},{4,5},{5,4},{6,7},{7,6},{8,9},{9,8},{10,11... | collective-permute-start | bytes 589832 | tf_op jit(solution)/shard_map/ppermute | solution.py:388
  16.1 1.3 %copy-start.4 = (s32[3840]{0:T(1024)S(1)}, s32[3840]{0:T(1024)}, u32[]{:S(2)}) copy-start(s32[3840]{0:T(1024)} %param.13) | copy-start | bytes 46084
  16.1 1.3 %copy-start.9 = (bf16[64,288]{1,0:T(8,128)(2,1)S(1)}, bf16[64,288]{1,0:T(8,128)(2,1)}, u32[]{:S(2)}) copy-start(bf16[64,288]{1,0:T(8,128)(2,1)} %constant.21.clone.table_ref) | copy-start | bytes 110596
  17.4 25.9 %copy-start.2 = (f32[6,128,128]{2,1,0:T(8,128)S(1)}, f32[6,128,128]{2,1,0:T(8,128)}, u32[]{:S(2)}) copy-start(f32[6,128,128]{2,1,0:T(8,128)} %inv_ref.1) | copy-start | bytes 1179652
  17.5 25.9 %copy-start.3 = (f32[5,128,128]{2,1,0:T(8,128)S(1)}, f32[5,128,128]{2,1,0:T(8,128)}, u32[]{:S(2)}) copy-start(f32[5,128,128]{2,1,0:T(8,128)} %mult_ref.1) | copy-start | bytes 983044
  19.8 51.7 %all-to-all-start = ((f32[256,1,384]{2,1,0:T(1,128)}), f32[256,1,384]{2,1,0:T(1,128)S(1)}, u32[]{:S(2)}, u32[]{:S(2)}) async-start(f32[256,1,384]{2,1,0:T(1,128)} %bitcast.5), calls=%async_computation | async-start | bytes 786432 | tf_op jit(solution)/shard_map/all_to_all | solution.py:384

commit v4 on v3

--- a/solution.py
+++ b/solution.py
@@ -20,7 +20,8 @@
 HALF = ROWS // 2
 SLOT = 48
 PADDED = 64
-JHALF = KEPT // 2
+HELD = PADDED // 2
+GAP = HELD - KEPT
 PARTS = 2 * ROWS * KEPT
 
 
@@ -28,10 +29,6 @@
     high = table.astype(np.float32).astype(BF16)
     low = (table - high.astype(np.float64)).astype(np.float32).astype(BF16)
     return high, low
-
-
-def place(jhalf, part):
-    return 32 * jhalf + 16 * part + jhalf
 
 
 def build_tables():
@@ -44,8 +41,8 @@
     short = 2.0 * np.pi * ((n1[:, None] * kept[None, :]) % OUTER) / OUTER
     to_grid = np.zeros((2 * SLOT, 64))
     scale = 1.0 / math.sqrt(modes)
-    re = np.array([place(j // half, 0) + j % half for j in range(KEPT)])
-    im = np.array([place(j // half, 1) + j % half for j in range(KEPT)])
+    re = np.arange(KEPT)
+    im = HELD + GAP + re
     to_grid[:OUTER, re] = np.cos(short) * scale
     to_grid[:OUTER, im] = -np.sin(short) * scale
     to_grid[SLOT : SLOT + OUTER, re] = np.sin(short) * scale
@@ -77,20 +74,19 @@
     )
 
 
-def call(kernel, out_shapes, args, name, scratch=(), scalars=0, flops=0, out_space=pltpu.VMEM):
-    shapes = [jax.ShapeDtypeStruct(*shape) if out_space is None else out_space(*shape) for shape in out_shapes]
+def call(kernel, out_shapes, args, name, scratch=(), scalars=0, flops=0, inputs=pltpu.VMEM, on_chip=True):
+    shapes = [pltpu.VMEM(*shape) if on_chip else jax.ShapeDtypeStruct(*shape) for shape in out_shapes]
     args = [
-        arg if i < scalars else pltpu.with_memory_space_constraint(arg, pltpu.VMEM)
+        arg if i < scalars else pltpu.with_memory_space_constraint(arg, inputs)
         for i, arg in enumerate(args)
     ]
     smem = pl.BlockSpec(memory_space=pltpu.SMEM)
-    vmem = pl.BlockSpec(memory_space=pltpu.VMEM)
     return pl.pallas_call(
         kernel,
         out_shape=shapes,
-        in_specs=[smem] * scalars + [vmem] * (len(args) - scalars),
-        out_specs=[vmem] * len(shapes),
-        scratch_shapes=[pltpu.VMEM(*shape) for shape in scratch],
+        in_specs=[smem] * scalars + [pl.BlockSpec(memory_space=inputs)] * (len(args) - scalars),
+        out_specs=[pl.BlockSpec(memory_space=pltpu.VMEM)] * len(shapes),
+        scratch_shapes=[pltpu.VMEM(*shape) if isinstance(shape, tuple) else shape for shape in scratch],
         compiler_params=pltpu.CompilerParams(vmem_limit_bytes=16 << 20),
         cost_estimate=pl.CostEstimate(flops=flops, bytes_accessed=1000000, transcendentals=0),
         name=name,
@@ -107,22 +103,40 @@
     return high, low
 
 
-def prepare_kernel(y_ref, a_ref, b_ref, send_ref, keep_ref):
+def prepare_kernel(y_ref, a_hbm, b_hbm, *refs):
+    count = (len(refs) - 5) // 2
+    tables, (send_ref, keep_ref), copied = refs[:count], refs[count : count + 2], refs[count + 2 : -3]
+    a_ref, b_ref, sems = refs[-3:]
+    pairs = [(a_hbm, a_ref), (b_hbm, b_ref), *zip(tables, copied)]
+    copies = [pltpu.make_async_copy(*pair, sems.at[i]) for i, pair in enumerate(pairs)]
+    for copy in copies:
+        copy.start()
     mine = y_ref[0]
+    for copy in copies[:2]:
+        copy.wait()
     for half, out_ref in ((1 - mine, send_ref), (mine, keep_ref)):
         for field, ref in enumerate((a_ref, b_ref)):
             for i in range(HALF):
+                base = half * (HALF * KEPT) + i * KEPT
                 row = (field * HALF + i) * PADDED
-                for jhalf in range(2):
-                    for part in range(2):
-                        base = half * (HALF * KEPT) + part * (PARTS // 2) + i * KEPT
-                        base = base + jhalf * (JHALF - 1)
-                        out_ref[pl.ds(row + 32 * jhalf + 16 * part, 16), :] = ref[pl.ds(base, 16), :]
-
-
-def prepare(y, field_a, field_b):
+                out_ref[pl.ds(row, HELD), :] = ref[pl.ds(base, HELD), :]
+                out_ref[pl.ds(row + HELD, HELD), :] = ref[pl.ds(base + PARTS // 2 - GAP, HELD), :]
+    for copy in copies[2:]:
+        copy.wait()
+
+
+def prepare(y, field_a, field_b, tables):
     shape = ((2 * HALF * PADDED, LANES), jnp.float32)
-    return call(prepare_kernel, [shape, shape], (y, field_a, field_b), "prepare", scalars=1)
+    send, own, *copied = call(
+        prepare_kernel,
+        [shape, shape] + [(table.shape, table.dtype) for table in tables.values()],
+        (y, field_a, field_b, *tables.values()),
+        "prepare",
+        scratch=[(field_a.shape, jnp.float32)] * 2 + [pltpu.SemaphoreType.DMA((2 + len(tables),))],
+        scalars=1,
+        inputs=pltpu.HBM,
+    )
+    return send, own, dict(zip(tables, copied))
 
 
 def load_modes(w_ref, field, i):
@@ -228,10 +242,9 @@
     table = table_ref[...]
     twr, twi = twr_ref[...], twi_ref[...]
     mask_ref[...] = jnp.zeros_like(mask_ref)
-    for jhalf in range(2):
-        for part in range(2):
-            flags = keep_ref[pl.ds(jhalf * JHALF, JHALF), :].astype(jnp.float32)
-            mask_ref[pl.ds(place(jhalf, part), JHALF), :] = flags
+    flags = keep_ref[...].astype(jnp.float32)
+    mask_ref[pl.ds(0, KEPT), :] = flags
+    mask_ref[pl.ds(HELD + GAP, KEPT), :] = flags
     mask = mask_ref[...]
 
     def updated(target, i):
@@ -254,22 +267,18 @@
             for field in range(2)
         ]
 
-    for i in range(HALF):
-        blocks = updated(0, i) + updated(1, i)
-        for jhalf in range(2):
-            columns = jnp.concatenate(
-                [block[32 * jhalf : 32 * jhalf + 32] for block in blocks], axis=0
-            )
-            out_ref[pl.ds(HALF * jhalf + i, LANES, stride=ROWS), :] = columns.T
-
-
-def to_rhs(x, grids, own, other, keep, tables):
+    for row in range(ROWS):
+        columns = jnp.concatenate(updated(row // HALF, row % HALF), axis=0)
+        out_ref[pl.ds(row, LANES, stride=ROWS), :] = columns.T
+
+
+def to_rhs(x, grids, own, other, tables):
     rows = 2 * ROWS * SLOT
-    names = ("to_modes", "twist_re", "twist_im", "lanes_h", "lanes_l")
+    names = ("keep", "to_modes", "twist_re", "twist_im", "lanes_h", "lanes_l")
     (rhs,) = call(
         modes_kernel,
         [((ROWS * LANES, LANES), jnp.float32)],
-        (x, *grids, own, other, keep, *[tables[name] for name in names]),
+        (x, *grids, own, other, *[tables[name] for name in names]),
         "to_rhs",
         scratch=[((rows, 2 * LANES), jnp.bfloat16)] * 2 + [((PADDED, LANES), jnp.float32)],
         scalars=1,
@@ -330,58 +339,42 @@
     )
 
 
-def solve_kernel(high_ref, low_ref, r_ref, out_ref, n_ref):
+def solve_kernel(high_ref, low_ref, r_ref, out_ref):
     high, low = split(r_ref[...])
     both = dot(high_ref[...], jnp.concatenate([high, low], axis=1))
-    n_ref[...] = both[:, :LANES] + both[:, LANES:] + dot(low_ref[...], high)
-    for i in range(HALF):
-        first = n_ref[pl.ds(i, LANES, stride=ROWS), :]
-        second = n_ref[pl.ds(HALF + i, LANES, stride=ROWS), :]
-        for target in range(2):
-            lanes = slice(target * 64, target * 64 + 64)
-            out_ref[pl.ds(HALF * target + i, LANES, stride=ROWS), :] = jnp.concatenate(
-                [first[:, lanes], second[:, lanes]], axis=1
-            )
+    out_ref[...] = both[:, :LANES] + both[:, LANES:] + dot(low_ref[...], high)
 
 
 def solve(operator, rhs):
-    size = rhs.shape[0]
     (solved,) = call(
         solve_kernel,
         [(rhs.shape, jnp.float32)],
         (*operator, rhs),
         "solve",
-        scratch=[(rhs.shape, jnp.float32)],
-        flops=2 * size * size * 256 * 2,
+        flops=2 * rhs.shape[0] ** 2 * 256 * 2,
     )
     return solved
 
 
 def spread_kernel(s_ref, a_ref, b_ref):
-    for jhalf in range(2):
-        for i in range(HALF):
-            columns = s_ref[pl.ds(HALF * jhalf + i, LANES, stride=ROWS), :].T
-            for second in range(2):
-                for field, ref in enumerate((a_ref, b_ref)):
-                    for part in range(2):
-                        start = second * 64 + field * 32 + part * 16 + jhalf
-                        row = part * (PARTS // 2) + (i + HALF * second) * KEPT + jhalf * JHALF
-                        ref[pl.ds(row, JHALF), :] = columns[start : start + JHALF]
+    for row in range(ROWS):
+        columns = s_ref[pl.ds(row, LANES, stride=ROWS), :].T
+        for field, ref in enumerate((a_ref, b_ref)):
+            base = field * PADDED
+            ref[pl.ds(row * KEPT, KEPT), :] = columns[base : base + KEPT]
+            base = base + HELD + GAP
+            ref[pl.ds(PARTS // 2 + row * KEPT, KEPT), :] = columns[base : base + KEPT]
 
 
 def spread(solved):
     return call(
-        spread_kernel, [((PARTS, LANES), jnp.float32)] * 2, (solved,), "spread", out_space=None
-    )
-
-
-ORDER = ("wa", "y")
-
-
-def exchange(rows):
-    count = 2 * LANES
+        spread_kernel, [((PARTS, LANES), jnp.float32)] * 2, (solved,), "spread", on_chip=False
+    )
+
+
+def exchange(rows, axes, count):
     sent = rows.reshape(count, 1, rows.size // count)
-    return lax.all_to_all(sent, ORDER, 0, 0, tiled=True).reshape(rows.shape)
+    return lax.all_to_all(sent, axes, 0, 0, tiled=True).reshape(rows.shape)
 
 
 def swap(value, axis):
@@ -390,18 +383,23 @@
 
 def body(field_a, field_b, keep_mask, block_inv, lower_mult):
     tables = {name: jnp.asarray(table) for name, table in build_tables().items()}
+    tables["keep"] = keep_mask.reshape(KEPT, LANES)
     y = lax.axis_index("y").astype(jnp.int32).reshape(1)
     x = 2 * y + lax.axis_index("c").astype(jnp.int32)
-    send, own = prepare(y, field_a.reshape(PARTS, LANES), field_b.reshape(PARTS, LANES))
+    fields = (field_a.reshape(PARTS, LANES), field_b.reshape(PARTS, LANES))
+    send, own, tables = prepare(y, *fields, tables)
+
     two = swap(send, "y")
+    first = to_grid(own, tables)
     one = swap(own, "c")
-    grids = [to_grid(own, tables), to_grid(one, tables)]
-    two, *grids = lax.optimization_barrier((two, *grids))
+    one, two, first = lax.optimization_barrier((one, two, first))
     three = swap(two, "c")
-    grids += [to_grid(two, tables), to_grid(three, tables)]
-    rhs = to_rhs(x, grids, own, two, keep_mask.reshape(KEPT, LANES), tables)
+    grids = (first, *[to_grid(part, tables) for part in (one, two, three)])
+
+    rhs = to_rhs(x, grids, own, two, tables)
     operator = solve_operator(block_inv, lower_mult)
-    new_a, new_b = spread(exchange(solve(operator, exchange(rhs))))
+    solved = solve(operator, exchange(rhs, ("wa", "y"), 2 * LANES))
+    new_a, new_b = spread(exchange(solved, "wa", LANES))
     return (new_a.reshape(field_a.shape), new_b.reshape(field_b.shape))
 
 

time: 112 us -> 107 us (0.955); the launches traced: 110 us -> 107 us
  local copies, waits for them, and re-layouts: 5.97 us -> 0.01 us
  waiting for transfers between devices: 26.4 us -> 28 us
  Pallas kernels: 9.18 us -> 10.3 us
    unnamed x32 -> x4, local copies, waits for them, and re-layouts: 5.97 us -> 0.01 us
    ppermute x3, waiting for transfers between devices: 1.49 us -> 3.15 us  [swap(): return lax.ppermute(value, axis, [(0, 1), (1, 0)])]
    pallas_call x9, Pallas kernels: 9.18 us -> 10.3 us  [call(): pl.pallas_call(kernel, out_shape=shapes, in_specs=[smem] * scalars + [pl....]
where the time goes in v4:
time: 107 us
  blocking collectives  36.8 us (34%)
  starting transfers between devices  30.8 us (29%)
  waiting for transfers between devices  28 us (26%)
  Pallas kernels  10.3 us (10%)
    all_to_all x1, blocking collectives, exchange(): return lax.all_to_all(sent, axes, 0, 0, tiled=True).reshape(rows.shape)  36.8 us
    all_to_all x1, waiting for transfers between devices, exchange(): return lax.all_to_all(sent, axes, 0, 0, tiled=True).reshape(rows.shape)  24.9 us
    all_to_all x1, starting transfers between devices, exchange(): return lax.all_to_all(sent, axes, 0, 0, tiled=True).reshape(rows.shape)  23.5 us
    pallas_call x9, Pallas kernels, call(): pl.pallas_call(kernel, out_shape=shapes, in_specs=[smem] * scalars + [pl....  10.3 us
    ppermute x3, starting transfers between devices, swap(): return lax.ppermute(value, axis, [(0, 1), (1, 0)])  7.32 us
    ppermute x3, waiting for transfers between devices, swap(): return lax.ppermute(value, axis, [(0, 1), (1, 0)])  3.15 us
  transfers between devices with their start and end apart: 4, of which 3 were waited for; matrix products, arithmetic and copies ran while one was open for 0% of the time, Pallas kernels for 4%

profile of v4, /device:TPU:6, one launch (start us, length us, event | category | flops | bytes accessed | tf_op | source)
XLA Modules:
  0.0 106.7 jit_solution(8985906259524189071)
XLA Ops:
  0.6 1.3 %prepare.1 = (f32[384,128]{1,0:T(8,128)S(1)}, f32[384,128]{1,0:T(8,128)S(1)}, bf16[96,192]{1,0:T(8,128)(2,1)S(1)}, bf16[64,288]{1,0:T(8,128)(2,1)S(1)}, f32[48,1...) custom-call(s32[1]{0:T(128)} %bitcast.y_ref, ...), custom_call_target="tpu_custom_call" | custom-call | bytes 1000000 | tf_op jit(solution)/shard_map/prepare/pallas_call | solution.py:84
  2.0 3.5 %collective-permute-start.1 = (f32[384,128]{1,0:T(8,128)S(1)}, f32[384,128]{1,0:T(8,128)S(1)}, u32[]{:S(2)}, u32[]{:S(2)}) collective-permute-start(f32[384,128]{1,0:T(8,128)S(1)} %get-tuple-element.21), channel_id=1, source_target_pairs={{0,2},{2,0},{1,3},{3,1},{4,6},{6,4},{5,7},{7,5},{8,10},{10,8},{9,1... | collective-permute-start | bytes 589832 | tf_op jit(solution)/shard_map/ppermute | solution.py:381
  5.5 1.9 %collective-permute-start = (f32[384,128]{1,0:T(8,128)S(1)}, f32[384,128]{1,0:T(8,128)S(1)}, u32[]{:S(2)}, u32[]{:S(2)}) collective-permute-start(f32[384,128]{1,0:T(8,128)S(1)} %get-tuple-element.20.w_ref.w0_ref), channel_id=1, source_target_pairs={{0,1},{1,0},{2,3},{3,2},{4,5},{5,4},{6,7},{7,6},{8,9},{9,8},{10,11... | collective-permute-start | bytes 589832 | tf_op jit(solution)/shard_map/ppermute | solution.py:381
  7.4 0.5 to_grid.4.g0
  7.8 2.7 %collective-permute-done.1.w_ref.w2_ref = f32[384,128]{1,0:T(8,128)S(1)} collective-permute-done((f32[384,128]{1,0:T(8,128)S(1)}, f32[384,128]{1,0:T(8,128)S(1)}, u32[]{:S(2)}, u32[]{:S(2)}) %collective-permute-start.1) | collective-permute-done | bytes 196640 | tf_op jit(solution)/shard_map/ppermute | solution.py:381
  10.5 0.0 collective-permute-done.w_ref
  10.5 1.9 %collective-permute-start.2 = (f32[384,128]{1,0:T(8,128)S(1)}, f32[384,128]{1,0:T(8,128)S(1)}, u32[]{:S(2)}, u32[]{:S(2)}) collective-permute-start(f32[384,128]{1,0:T(8,128)S(1)} %collective-permute-done.1.w_ref.w2_ref), channel_id=1, source_target_pairs={{0,1},{1,0},{2,3},{3,2},{4,5},{5,4},{6,7},{7,6},{8,9},{9,8},{10,11... | collective-permute-start | bytes 589832 | tf_op jit(solution)/shard_map/ppermute | solution.py:381
  12.4 0.5 to_grid.6.g2
  12.9 0.4 to_grid.5.g1
  13.3 0.5 collective-permute-done.2.w_ref
  13.8 0.4 to_grid.7.g3
  14.3 0.0 copy-start
  14.3 0.0 copy-start.1
  14.3 2.3 %to_rhs.1 = f32[768,128]{1,0:T(8,128)} custom-call(s32[1]{0:T(128)S(6)} %add.7.x_ref, f32[288,256]{1,0:T(8,128)S(1)} %to_grid.4.g0, f32[288,256]{1,0:T(8,128)S(1)} %to_grid.5.g1, f32[288,256]{1,0:T(8,128)S(1)} %to_grid.6.g2, f32[288,256]{1,0:T(8,128)S(1)} %to_grid.7.g3, f32[384,128]{1,0:T(8,128)S(1)} %get-tuple-element.20.w_ref.w0_ref, ...), custom_call_target="tpu_custom_call" | custom-call | flops 905969664 | bytes 1000000 | tf_op jit(solution)/shard_map/to_rhs/pallas_call | solution.py:84
  16.6 23.5 %all-to-all-start = ((f32[256,1,384]{2,1,0:T(1,128)}), f32[256,1,384]{2,1,0:T(1,128)S(1)}, u32[]{:S(2)}, u32[]{:S(2)}) async-start(f32[256,1,384]{2,1,0:T(1,128)} %bitcast.5), calls=%async_computation | async-start | bytes 786432 | tf_op jit(solution)/shard_map/all_to_all | solution.py:377
  40.1 0.0 copy-done
  40.2 0.0 copy-done.1
  40.2 3.2 %solve_operator.1 = (bf16[768,768]{1,0:T(8,128)(2,1)S(1)}, bf16[768,768]{1,0:T(8,128)(2,1)S(1)}) custom-call(f32[6,128,128]{2,1,0:T(8,128)S(1)} %copy-done, f32[5,128,128]{2,1,0:T(8,128)S(1)} %copy-done.1), custom_call_target="tpu_custom_call" | custom-call | flops 2768240640 | bytes 1000000 | tf_op jit(solution)/shard_map/solve_operator/pallas_call | solution.py:84
  43.4 24.9 %all-to-all-done = f32[256,1,384]{2,1,0:T(1,128)S(1)} async-done(((f32[256,1,384]{2,1,0:T(1,128)}), f32[256,1,384]{2,1,0:T(1,128)S(1)}, u32[]{:S(2)}, u32[]{:S(2)}) %all-to-all-start) | async-done | bytes 393248 | tf_op jit(solution)/shard_map/all_to_all | solution.py:377
  68.2 0.8 solve.1
  69.0 36.8 %all_to_all.10 = f32[128,1,768]{2,1,0:T(1,128)S(1)} all-to-all(f32[128,1,768]{2,1,0:T(1,128)S(1)} %bitcast.12), channel_id=1, replica_groups=mesh['wa'=128,'y'=2,'c'=2] {'wa'}, dimensions={0} | all-to-all | bytes 786432 | tf_op jit(solution)/shard_map/all_to_all | solution.py:377
  105.8 0.9 spread.1
Async XLA Ops:
  2.0 8.5 %collective-permute-start.1 = (f32[384,128]{1,0:T(8,128)S(1)}, f32[384,128]{1,0:T(8,128)S(1)}, u32[]{:S(2)}, u32[]{:S(2)}) collective-permute-start(f32[384,128]{1,0:T(8,128)S(1)} %get-tuple-element.21), channel_id=1, source_target_pairs={{0,2},{2,0},{1,3},{3,1},{4,6},{6,4},{5,7},{7,5},{8,10},{10,8},{9,1... | collective-permute-start | bytes 589832 | tf_op jit(solution)/shard_map/ppermute | solution.py:381
  5.5 5.0 %collective-permute-start = (f32[384,128]{1,0:T(8,128)S(1)}, f32[384,128]{1,0:T(8,128)S(1)}, u32[]{:S(2)}, u32[]{:S(2)}) collective-permute-start(f32[384,128]{1,0:T(8,128)S(1)} %get-tuple-element.20.w_ref.w0_ref), channel_id=1, source_target_pairs={{0,1},{1,0},{2,3},{3,2},{4,5},{5,4},{6,7},{7,6},{8,9},{9,8},{10,11... | collective-permute-start | bytes 589832 | tf_op jit(solution)/shard_map/ppermute | solution.py:381
  10.5 3.3 %collective-permute-start.2 = (f32[384,128]{1,0:T(8,128)S(1)}, f32[384,128]{1,0:T(8,128)S(1)}, u32[]{:S(2)}, u32[]{:S(2)}) collective-permute-start(f32[384,128]{1,0:T(8,128)S(1)} %collective-permute-done.1.w_ref.w2_ref), channel_id=1, source_target_pairs={{0,1},{1,0},{2,3},{3,2},{4,5},{5,4},{6,7},{7,6},{8,9},{9,8},{10,11... | collective-permute-start | bytes 589832 | tf_op jit(solution)/shard_map/ppermute | solution.py:381
  14.3 25.9 %copy-start = (f32[6,128,128]{2,1,0:T(8,128)S(1)}, f32[6,128,128]{2,1,0:T(8,128)}, u32[]{:S(2)}) copy-start(f32[6,128,128]{2,1,0:T(8,128)} %inv_ref.1) | copy-start | bytes 1179652
  14.3 25.9 %copy-start.1 = (f32[5,128,128]{2,1,0:T(8,128)S(1)}, f32[5,128,128]{2,1,0:T(8,128)}, u32[]{:S(2)}) copy-start(f32[5,128,128]{2,1,0:T(8,128)} %mult_ref.1) | copy-start | bytes 983044
  16.6 51.6 %all-to-all-start = ((f32[256,1,384]{2,1,0:T(1,128)}), f32[256,1,384]{2,1,0:T(1,128)S(1)}, u32[]{:S(2)}, u32[]{:S(2)}) async-start(f32[256,1,384]{2,1,0:T(1,128)} %bitcast.5), calls=%async_computation | async-start | bytes 786432 | tf_op jit(solution)/shard_map/all_to_all | solution.py:377

commit v5 on v4

--- a/solution.py
+++ b/solution.py
@@ -1,3 +1,4 @@
+import functools
 import math
 
 import jax
@@ -23,6 +24,7 @@
 HELD = PADDED // 2
 GAP = HELD - KEPT
 PARTS = 2 * ROWS * KEPT
+BLOCKS = (2 * HALF * PADDED, LANES)
 
 
 def split_np(table):
@@ -76,15 +78,13 @@
 
 def call(kernel, out_shapes, args, name, scratch=(), scalars=0, flops=0, inputs=pltpu.VMEM, on_chip=True):
     shapes = [pltpu.VMEM(*shape) if on_chip else jax.ShapeDtypeStruct(*shape) for shape in out_shapes]
-    args = [
-        arg if i < scalars else pltpu.with_memory_space_constraint(arg, inputs)
-        for i, arg in enumerate(args)
-    ]
-    smem = pl.BlockSpec(memory_space=pltpu.SMEM)
+    spaces = inputs if isinstance(inputs, list) else [inputs] * (len(args) - scalars)
+    args = [*args[:scalars], *map(pltpu.with_memory_space_constraint, args[scalars:], spaces)]
+    specs = [pl.BlockSpec(memory_space=space) for space in [pltpu.SMEM] * scalars + spaces]
     return pl.pallas_call(
         kernel,
         out_shape=shapes,
-        in_specs=[smem] * scalars + [pl.BlockSpec(memory_space=inputs)] * (len(args) - scalars),
+        in_specs=specs,
         out_specs=[pl.BlockSpec(memory_space=pltpu.VMEM)] * len(shapes),
         scratch_shapes=[pltpu.VMEM(*shape) if isinstance(shape, tuple) else shape for shape in scratch],
         compiler_params=pltpu.CompilerParams(vmem_limit_bytes=16 << 20),
@@ -103,40 +103,64 @@
     return high, low
 
 
-def prepare_kernel(y_ref, a_hbm, b_hbm, *refs):
-    count = (len(refs) - 5) // 2
-    tables, (send_ref, keep_ref), copied = refs[:count], refs[count : count + 2], refs[count + 2 : -3]
-    a_ref, b_ref, sems = refs[-3:]
-    pairs = [(a_hbm, a_ref), (b_hbm, b_ref), *zip(tables, copied)]
-    copies = [pltpu.make_async_copy(*pair, sems.at[i]) for i, pair in enumerate(pairs)]
+def pad_half(out_ref, refs, half):
+    for field, ref in enumerate(refs):
+        for i in range(HALF):
+            base = half * (HALF * KEPT) + i * KEPT
+            row = (field * HALF + i) * PADDED
+            out_ref[pl.ds(row, HELD), :] = ref[pl.ds(base, HELD), :]
+            out_ref[pl.ds(row + HELD, HELD), :] = ref[pl.ds(base + PARTS // 2 - GAP, HELD), :]
+
+
+def send_kernel(y_ref, a_hbm, b_hbm, send_ref, a_ref, b_ref, sems):
+    copies = [
+        pltpu.make_async_copy(*pair, sems.at[i])
+        for i, pair in enumerate([(a_hbm, a_ref), (b_hbm, b_ref)])
+    ]
     for copy in copies:
         copy.start()
-    mine = y_ref[0]
-    for copy in copies[:2]:
+    for copy in copies:
         copy.wait()
-    for half, out_ref in ((1 - mine, send_ref), (mine, keep_ref)):
-        for field, ref in enumerate((a_ref, b_ref)):
-            for i in range(HALF):
-                base = half * (HALF * KEPT) + i * KEPT
-                row = (field * HALF + i) * PADDED
-                out_ref[pl.ds(row, HELD), :] = ref[pl.ds(base, HELD), :]
-                out_ref[pl.ds(row + HELD, HELD), :] = ref[pl.ds(base + PARTS // 2 - GAP, HELD), :]
-    for copy in copies[2:]:
-        copy.wait()
-
-
-def prepare(y, field_a, field_b, tables):
-    shape = ((2 * HALF * PADDED, LANES), jnp.float32)
-    send, own, *copied = call(
-        prepare_kernel,
-        [shape, shape] + [(table.shape, table.dtype) for table in tables.values()],
-        (y, field_a, field_b, *tables.values()),
-        "prepare",
-        scratch=[(field_a.shape, jnp.float32)] * 2 + [pltpu.SemaphoreType.DMA((2 + len(tables),))],
+    pad_half(send_ref, (a_ref, b_ref), 1 - y_ref[0])
+
+
+def send_half(y, field_a, field_b):
+    return call(
+        send_kernel,
+        [(BLOCKS, jnp.float32)] + [(field_a.shape, jnp.float32)] * 2,
+        (y, field_a, field_b),
+        "send_half",
+        scratch=[pltpu.SemaphoreType.DMA((2,))],
         scalars=1,
         inputs=pltpu.HBM,
     )
-    return send, own, dict(zip(tables, copied))
+
+
+def keep_kernel(y_ref, *refs):
+    count = (len(refs) - 4) // 2
+    a_ref, b_ref, tables = refs[count], refs[count + 1], refs[:count]
+    keep_ref, copied, sems = refs[count + 2], refs[count + 3 : -1], refs[-1]
+    copies = [
+        pltpu.make_async_copy(*pair, sems.at[i]) for i, pair in enumerate(zip(tables, copied))
+    ]
+    for copy in copies:
+        copy.start()
+    pad_half(keep_ref, (a_ref, b_ref), y_ref[0])
+    for copy in copies:
+        copy.wait()
+
+
+def keep_half(y, field_a, field_b, tables):
+    own, *copied = call(
+        keep_kernel,
+        [(BLOCKS, jnp.float32)] + [(table.shape, table.dtype) for table in tables.values()],
+        (y, *tables.values(), field_a, field_b),
+        "keep_half",
+        scratch=[pltpu.SemaphoreType.DMA((len(tables),))],
+        scalars=1,
+        inputs=[pltpu.HBM] * len(tables) + [pltpu.VMEM] * 2,
+    )
+    return own, dict(zip(tables, copied))
 
 
 def load_modes(w_ref, field, i):
@@ -190,6 +214,18 @@
     return (left[0] * right[0] - left[1] * right[1], left[0] * right[1] + left[1] * right[0])
 
 
+def plus(left, right):
+    return (left[0] + right[0], left[1] + right[1])
+
+
+def minus(left, right):
+    return (left[0] - right[0], left[1] - right[1])
+
+
+def add(terms):
+    return functools.reduce(plus, terms)
+
+
 def modes_kernel(
     x_ref, g0, g1, g2, g3, w0_ref, w2_ref, keep_ref, table_ref, twr_ref, twi_ref, lh_ref, ll_ref,
     out_ref, uh_ref, ul_ref, mask_ref,
@@ -211,17 +247,16 @@
             a = [load(grid, 0) for grid in grids]
             b = [load(grid, 1) for grid in grids]
             for target, pairs in enumerate(all_pairs):
-                p = q = None
+                p = add([complex_product(a[left], b[right]) for left, right in pairs])
+                terms = []
                 for left, right in pairs:
-                    ab = complex_product(a[left], b[right])
-                    aa = complex_product(a[left], a[right])
-                    bb = complex_product(b[left], b[right])
-                    if p is None:
-                        p = ab
-                        q = (aa[0] - bb[0], aa[1] - bb[1])
-                    else:
-                        p = (p[0] + ab[0], p[1] + ab[1])
-                        q = (q[0] + aa[0] - bb[0], q[1] + aa[1] - bb[1])
+                    if left == right:
+                        terms.append(complex_product(minus(a[left], b[left]), plus(a[left], b[left])))
+                    elif left < right:
+                        aa = complex_product(a[left], a[right])
+                        both = minus(aa, complex_product(b[left], b[right]))
+                        terms.append(plus(both, both))
+                q = add(terms)
                 for field, (re, im) in enumerate((p, q)):
                     high, low = split(jnp.concatenate([re, -im], axis=1))
                     start = base + (target * 2 * HALF + field) * SLOT
@@ -232,11 +267,11 @@
 
         lax.fori_loop(0, 3 * HALF, step, 0)
 
-    for value in range(4):
-
-        @pl.when(x == value)
-        def _(value=value):
-            convolve([pairs_of(value, 2 * target + value % 2) for target in range(2)])
+    for odd in range(2):
+
+        @pl.when(x % 2 == odd)
+        def _(odd=odd):
+            convolve([pairs_of(odd, 2 * target + odd) for target in range(2)])
 
     spectra = lane_transform(uh_ref, ul_ref, lh_ref, ll_ref)
     table = table_ref[...]
@@ -387,7 +422,8 @@
     y = lax.axis_index("y").astype(jnp.int32).reshape(1)
     x = 2 * y + lax.axis_index("c").astype(jnp.int32)
     fields = (field_a.reshape(PARTS, LANES), field_b.reshape(PARTS, LANES))
-    send, own, tables = prepare(y, *fields, tables)
+    send, *fields = send_half(y, *fields)
+    own, tables = keep_half(y, *fields, tables)
 
     two = swap(send, "y")
     first = to_grid(own, tables)

time: 107 us -> 107 us (level)
    ppermute x3, waiting for transfers between devices: 3.15 us -> 2 us  [swap(): return lax.ppermute(value, axis, [(0, 1), (1, 0)])]
    pallas_call x9 -> x10, Pallas kernels: 10.3 us -> 11.1 us  [call(): pl.pallas_call(kernel, out_shape=shapes, in_specs=specs, out_specs=[pl.Bl...]
  transfers between devices with their start and end apart: 4 -> 4, of which waited for: 3 -> 3; matrix products, arithmetic and copies ran while one was open for 0% -> 0% of each run, Pallas kernels for 4% -> 5%
where the time goes in v5:
time: 107 us; the launch traced here: 106 us
  blocking collectives  36.6 us (34%)
  starting transfers between devices  30.8 us (29%)
  waiting for transfers between devices  27 us (25%)
  Pallas kernels  11.1 us (10%)
    all_to_all x1, blocking collectives, exchange(): return lax.all_to_all(sent, axes, 0, 0, tiled=True).reshape(rows.shape)  36.6 us
    all_to_all x1, waiting for transfers between devices, exchange(): return lax.all_to_all(sent, axes, 0, 0, tiled=True).reshape(rows.shape)  25 us
    all_to_all x1, starting transfers between devices, exchange(): return lax.all_to_all(sent, axes, 0, 0, tiled=True).reshape(rows.shape)  23.5 us
    pallas_call x10, Pallas kernels, call(): pl.pallas_call(kernel, out_shape=shapes, in_specs=specs, out_specs=[pl.Bl...  11.1 us
    ppermute x3, starting transfers between devices, swap(): return lax.ppermute(value, axis, [(0, 1), (1, 0)])  7.32 us
  transfers between devices with their start and end apart: 4, of which 3 were waited for; matrix products, arithmetic and copies ran while one was open for 0% of the time, Pallas kernels for 5%

profile of v5, /device:TPU:6, one launch (start us, length us, event | category | flops | bytes accessed | tf_op | source)
XLA Modules:
  0.0 106.4 jit_solution(17135555186618744483)
XLA Ops:
  0.6 1.0 send_half.1
  1.7 3.5 %collective-permute-start.1 = (f32[384,128]{1,0:T(8,128)S(1)}, f32[384,128]{1,0:T(8,128)S(1)}, u32[]{:S(2)}, u32[]{:S(2)}) collective-permute-start(f32[384,128]{1,0:T(8,128)S(1)} %get-tuple-element.25), channel_id=1, source_target_pairs={{0,2},{2,0},{1,3},{3,1},{4,6},{6,4},{5,7},{7,5},{8,10},{10,8},{9,1... | collective-permute-start | bytes 589832 | tf_op jit(solution)/shard_map/ppermute | solution.py:416
  5.2 1.1 %keep_half.1 = (f32[384,128]{1,0:T(8,128)S(1)}, bf16[96,192]{1,0:T(8,128)(2,1)S(1)}, bf16[64,288]{1,0:T(8,128)(2,1)S(1)}, f32[48,128]{1,0:T(8,128)S(1)}, f32[48,...) custom-call(s32[1]{0:T(128)} %bitcast.y_ref, ...), custom_call_target="tpu_custom_call" | custom-call | bytes 1000000 | tf_op jit(solution)/shard_map/keep_half/pallas_call | solution.py:84
  6.3 1.9 %collective-permute-start = (f32[384,128]{1,0:T(8,128)S(1)}, f32[384,128]{1,0:T(8,128)S(1)}, u32[]{:S(2)}, u32[]{:S(2)}) collective-permute-start(f32[384,128]{1,0:T(8,128)S(1)} %get-tuple-element.24.w_ref.w0_ref), channel_id=1, source_target_pairs={{0,1},{1,0},{2,3},{3,2},{4,5},{5,4},{6,7},{7,6},{8,9},{9,8},{10,11... | collective-permute-start | bytes 589832 | tf_op jit(solution)/shard_map/ppermute | solution.py:416
  8.2 0.5 to_grid.4.g0
  8.7 1.5 %collective-permute-done.1.w_ref.w2_ref = f32[384,128]{1,0:T(8,128)S(1)} collective-permute-done((f32[384,128]{1,0:T(8,128)S(1)}, f32[384,128]{1,0:T(8,128)S(1)}, u32[]{:S(2)}, u32[]{:S(2)}) %collective-permute-start.1) | collective-permute-done | bytes 196640 | tf_op jit(solution)/shard_map/ppermute | solution.py:416
  10.2 0.0 collective-permute-done.w_ref
  10.2 1.9 %collective-permute-start.2 = (f32[384,128]{1,0:T(8,128)S(1)}, f32[384,128]{1,0:T(8,128)S(1)}, u32[]{:S(2)}, u32[]{:S(2)}) collective-permute-start(f32[384,128]{1,0:T(8,128)S(1)} %collective-permute-done.1.w_ref.w2_ref), channel_id=1, source_target_pairs={{0,1},{1,0},{2,3},{3,2},{4,5},{5,4},{6,7},{7,6},{8,9},{9,8},{10,11... | collective-permute-start | bytes 589832 | tf_op jit(solution)/shard_map/ppermute | solution.py:416
  12.2 0.4 to_grid.6.g2
  12.6 0.5 to_grid.5.g1
  13.1 0.5 collective-permute-done.2.w_ref
  13.6 0.4 to_grid.7.g3
  14.0 0.0 copy-start
  14.0 0.0 copy-start.1
  14.0 2.3 %to_rhs.1 = f32[768,128]{1,0:T(8,128)} custom-call(s32[1]{0:T(128)S(6)} %add.7.x_ref, f32[288,256]{1,0:T(8,128)S(1)} %to_grid.4.g0, f32[288,256]{1,0:T(8,128)S(1)} %to_grid.5.g1, f32[288,256]{1,0:T(8,128)S(1)} %to_grid.6.g2, f32[288,256]{1,0:T(8,128)S(1)} %to_grid.7.g3, f32[384,128]{1,0:T(8,128)S(1)} %get-tuple-element.24.w_ref.w0_ref, ...), custom_call_target="tpu_custom_call" | custom-call | flops 905969664 | bytes 1000000 | tf_op jit(solution)/shard_map/to_rhs/pallas_call | solution.py:84
  16.3 23.5 %all-to-all-start = ((f32[256,1,384]{2,1,0:T(1,128)}), f32[256,1,384]{2,1,0:T(1,128)S(1)}, u32[]{:S(2)}, u32[]{:S(2)}) async-start(f32[256,1,384]{2,1,0:T(1,128)} %bitcast.5), calls=%async_computation | async-start | bytes 786432 | tf_op jit(solution)/shard_map/all_to_all | solution.py:412
  39.8 0.0 copy-done
  39.8 0.0 copy-done.1
  39.9 3.2 %solve_operator.1 = (bf16[768,768]{1,0:T(8,128)(2,1)S(1)}, bf16[768,768]{1,0:T(8,128)(2,1)S(1)}) custom-call(f32[6,128,128]{2,1,0:T(8,128)S(1)} %copy-done, f32[5,128,128]{2,1,0:T(8,128)S(1)} %copy-done.1), custom_call_target="tpu_custom_call" | custom-call | flops 2768240640 | bytes 1000000 | tf_op jit(solution)/shard_map/solve_operator/pallas_call | solution.py:84
  43.1 25.0 %all-to-all-done = f32[256,1,384]{2,1,0:T(1,128)S(1)} async-done(((f32[256,1,384]{2,1,0:T(1,128)}), f32[256,1,384]{2,1,0:T(1,128)S(1)}, u32[]{:S(2)}, u32[]{:S(2)}) %all-to-all-start) | async-done | bytes 393248 | tf_op jit(solution)/shard_map/all_to_all | solution.py:412
  68.1 0.8 solve.1
  68.9 36.6 %all_to_all.10 = f32[128,1,768]{2,1,0:T(1,128)S(1)} all-to-all(f32[128,1,768]{2,1,0:T(1,128)S(1)} %bitcast.12), channel_id=1, replica_groups=mesh['wa'=128,'y'=2,'c'=2] {'wa'}, dimensions={0} | all-to-all | bytes 786432 | tf_op jit(solution)/shard_map/all_to_all | solution.py:412
  105.5 0.9 spread.1
Async XLA Ops:
  1.7 8.5 %collective-permute-start.1 = (f32[384,128]{1,0:T(8,128)S(1)}, f32[384,128]{1,0:T(8,128)S(1)}, u32[]{:S(2)}, u32[]{:S(2)}) collective-permute-start(f32[384,128]{1,0:T(8,128)S(1)} %get-tuple-element.25), channel_id=1, source_target_pairs={{0,2},{2,0},{1,3},{3,1},{4,6},{6,4},{5,7},{7,5},{8,10},{10,8},{9,1... | collective-permute-start | bytes 589832 | tf_op jit(solution)/shard_map/ppermute | solution.py:416
  6.3 3.9 %collective-permute-start = (f32[384,128]{1,0:T(8,128)S(1)}, f32[384,128]{1,0:T(8,128)S(1)}, u32[]{:S(2)}, u32[]{:S(2)}) collective-permute-start(f32[384,128]{1,0:T(8,128)S(1)} %get-tuple-element.24.w_ref.w0_ref), channel_id=1, source_target_pairs={{0,1},{1,0},{2,3},{3,2},{4,5},{5,4},{6,7},{7,6},{8,9},{9,8},{10,11... | collective-permute-start | bytes 589832 | tf_op jit(solution)/shard_map/ppermute | solution.py:416
  10.2 3.3 %collective-permute-start.2 = (f32[384,128]{1,0:T(8,128)S(1)}, f32[384,128]{1,0:T(8,128)S(1)}, u32[]{:S(2)}, u32[]{:S(2)}) collective-permute-start(f32[384,128]{1,0:T(8,128)S(1)} %collective-permute-done.1.w_ref.w2_ref), channel_id=1, source_target_pairs={{0,1},{1,0},{2,3},{3,2},{4,5},{5,4},{6,7},{7,6},{8,9},{9,8},{10,11... | collective-permute-start | bytes 589832 | tf_op jit(solution)/shard_map/ppermute | solution.py:416
  14.0 25.8 %copy-start = (f32[6,128,128]{2,1,0:T(8,128)S(1)}, f32[6,128,128]{2,1,0:T(8,128)}, u32[]{:S(2)}) copy-start(f32[6,128,128]{2,1,0:T(8,128)} %inv_ref.1) | copy-start | bytes 1179652
  14.0 25.8 %copy-start.1 = (f32[5,128,128]{2,1,0:T(8,128)S(1)}, f32[5,128,128]{2,1,0:T(8,128)}, u32[]{:S(2)}) copy-start(f32[5,128,128]{2,1,0:T(8,128)} %mult_ref.1) | copy-start | bytes 983044
  16.3 51.8 %all-to-all-start = ((f32[256,1,384]{2,1,0:T(1,128)}), f32[256,1,384]{2,1,0:T(1,128)S(1)}, u32[]{:S(2)}, u32[]{:S(2)}) async-start(f32[256,1,384]{2,1,0:T(1,128)} %bitcast.5), calls=%async_computation | async-start | bytes 786432 | tf_op jit(solution)/shard_map/all_to_all | solution.py:412

commit v6 on v5

--- a/solution.py
+++ b/solution.py
@@ -68,7 +68,7 @@
     lanes_h, lanes_l = split_np(lanes)
     return dict(
         to_grid=np.concatenate([grid_h, grid_h, grid_l], axis=1),
-        to_modes=np.concatenate([modes_h, modes_h, modes_l], axis=1),
+        to_modes=np.block([[modes_h, modes_h], [modes_l, np.zeros_like(modes_l)]]),
         twist_re=twist_re,
         twist_im=twist_im,
         lanes_h=lanes_h,
@@ -294,7 +294,8 @@
             [jnp.concatenate(re_parts, axis=1), jnp.concatenate(im_parts, axis=1)], axis=0
         )
         high, low = split(twisted)
-        hat = dot(table, jnp.concatenate([high, low, high], axis=0))
+        hat = dot(table, jnp.concatenate([high, low], axis=0))
+        hat = hat[:PADDED] + hat[PADDED:]
         mine = (x // 2) == target
         return [
             jnp.where(mine, load_modes(w0_ref, field, i), load_modes(w2_ref, field, i))

time: 107 us -> 107 us (level)
  no operation moved by 1% of the time
where the time goes in v6:
time: 107 us; the launch traced here: 106 us
  blocking collectives  36.6 us (34%)
  starting transfers between devices  30.8 us (29%)
  waiting for transfers between devices  27 us (25%)
  Pallas kernels  11.1 us (10%)
    all_to_all x1, blocking collectives, exchange(): return lax.all_to_all(sent, axes, 0, 0, tiled=True).reshape(rows.shape)  36.6 us
    all_to_all x1, waiting for transfers between devices, exchange(): return lax.all_to_all(sent, axes, 0, 0, tiled=True).reshape(rows.shape)  25 us
    all_to_all x1, starting transfers between devices, exchange(): return lax.all_to_all(sent, axes, 0, 0, tiled=True).reshape(rows.shape)  23.5 us
    pallas_call x10, Pallas kernels, call(): pl.pallas_call(kernel, out_shape=shapes, in_specs=specs, out_specs=[pl.Bl...  11.1 us
    ppermute x3, starting transfers between devices, swap(): return lax.ppermute(value, axis, [(0, 1), (1, 0)])  7.32 us
  transfers between devices with their start and end apart: 4, of which 3 were waited for; matrix products, arithmetic and copies ran while one was open for 0% of the time, Pallas kernels for 5%

profile of v6, /device:TPU:6, one launch (start us, length us, event | category | flops | bytes accessed | tf_op | source)
XLA Modules:
  0.0 106.4 jit_solution(611147810999955679)
XLA Ops:
  0.6 1.0 send_half.1
  1.7 3.5 %collective-permute-start.1 = (f32[384,128]{1,0:T(8,128)S(1)}, f32[384,128]{1,0:T(8,128)S(1)}, u32[]{:S(2)}, u32[]{:S(2)}) collective-permute-start(f32[384,128]{1,0:T(8,128)S(1)} %get-tuple-element.25), channel_id=1, source_target_pairs={{0,2},{2,0},{1,3},{3,1},{4,6},{6,4},{5,7},{7,5},{8,10},{10,8},{9,1... | collective-permute-start | bytes 589832 | tf_op jit(solution)/shard_map/ppermute | solution.py:417
  5.2 1.1 %keep_half.1 = (f32[384,128]{1,0:T(8,128)S(1)}, bf16[96,192]{1,0:T(8,128)(2,1)S(1)}, bf16[128,192]{1,0:T(8,128)(2,1)S(1)}, f32[48,128]{1,0:T(8,128)S(1)}, f32[48...) custom-call(s32[1]{0:T(128)} %bitcast.y_ref, ...), custom_call_target="tpu_custom_call" | custom-call | bytes 1000000 | tf_op jit(solution)/shard_map/keep_half/pallas_call | solution.py:84
  6.3 1.9 %collective-permute-start = (f32[384,128]{1,0:T(8,128)S(1)}, f32[384,128]{1,0:T(8,128)S(1)}, u32[]{:S(2)}, u32[]{:S(2)}) collective-permute-start(f32[384,128]{1,0:T(8,128)S(1)} %get-tuple-element.24.w_ref.w0_ref), channel_id=1, source_target_pairs={{0,1},{1,0},{2,3},{3,2},{4,5},{5,4},{6,7},{7,6},{8,9},{9,8},{10,11... | collective-permute-start | bytes 589832 | tf_op jit(solution)/shard_map/ppermute | solution.py:417
  8.3 0.4 to_grid.4.g0
  8.7 1.5 %collective-permute-done.1.w_ref.w2_ref = f32[384,128]{1,0:T(8,128)S(1)} collective-permute-done((f32[384,128]{1,0:T(8,128)S(1)}, f32[384,128]{1,0:T(8,128)S(1)}, u32[]{:S(2)}, u32[]{:S(2)}) %collective-permute-start.1) | collective-permute-done | bytes 196640 | tf_op jit(solution)/shard_map/ppermute | solution.py:417
  10.2 0.0 collective-permute-done.w_ref
  10.2 1.9 %collective-permute-start.2 = (f32[384,128]{1,0:T(8,128)S(1)}, f32[384,128]{1,0:T(8,128)S(1)}, u32[]{:S(2)}, u32[]{:S(2)}) collective-permute-start(f32[384,128]{1,0:T(8,128)S(1)} %collective-permute-done.1.w_ref.w2_ref), channel_id=1, source_target_pairs={{0,1},{1,0},{2,3},{3,2},{4,5},{5,4},{6,7},{7,6},{8,9},{9,8},{10,11... | collective-permute-start | bytes 589832 | tf_op jit(solution)/shard_map/ppermute | solution.py:417
  12.2 0.4 to_grid.6.g2
  12.6 0.5 to_grid.5.g1
  13.1 0.5 collective-permute-done.2.w_ref
  13.6 0.4 to_grid.7.g3
  14.0 0.0 copy-start
  14.0 0.0 copy-start.1
  14.0 2.3 %to_rhs.1 = f32[768,128]{1,0:T(8,128)} custom-call(s32[1]{0:T(128)S(6)} %add.7.x_ref, f32[288,256]{1,0:T(8,128)S(1)} %to_grid.4.g0, f32[288,256]{1,0:T(8,128)S(1)} %to_grid.5.g1, f32[288,256]{1,0:T(8,128)S(1)} %to_grid.6.g2, f32[288,256]{1,0:T(8,128)S(1)} %to_grid.7.g3, f32[384,128]{1,0:T(8,128)S(1)} %get-tuple-element.24.w_ref.w0_ref, ...), custom_call_target="tpu_custom_call" | custom-call | flops 905969664 | bytes 1000000 | tf_op jit(solution)/shard_map/to_rhs/pallas_call | solution.py:84
  16.3 23.5 %all-to-all-start = ((f32[256,1,384]{2,1,0:T(1,128)}), f32[256,1,384]{2,1,0:T(1,128)S(1)}, u32[]{:S(2)}, u32[]{:S(2)}) async-start(f32[256,1,384]{2,1,0:T(1,128)} %bitcast.5), calls=%async_computation | async-start | bytes 786432 | tf_op jit(solution)/shard_map/all_to_all | solution.py:413
  39.8 0.0 copy-done
  39.8 0.0 copy-done.1
  39.8 3.2 %solve_operator.1 = (bf16[768,768]{1,0:T(8,128)(2,1)S(1)}, bf16[768,768]{1,0:T(8,128)(2,1)S(1)}) custom-call(f32[6,128,128]{2,1,0:T(8,128)S(1)} %copy-done, f32[5,128,128]{2,1,0:T(8,128)S(1)} %copy-done.1), custom_call_target="tpu_custom_call" | custom-call | flops 2768240640 | bytes 1000000 | tf_op jit(solution)/shard_map/solve_operator/pallas_call | solution.py:84
  43.1 25.0 %all-to-all-done = f32[256,1,384]{2,1,0:T(1,128)S(1)} async-done(((f32[256,1,384]{2,1,0:T(1,128)}), f32[256,1,384]{2,1,0:T(1,128)S(1)}, u32[]{:S(2)}, u32[]{:S(2)}) %all-to-all-start) | async-done | bytes 393248 | tf_op jit(solution)/shard_map/all_to_all | solution.py:413
  68.0 0.8 solve.1
  68.8 36.6 %all_to_all.10 = f32[128,1,768]{2,1,0:T(1,128)S(1)} all-to-all(f32[128,1,768]{2,1,0:T(1,128)S(1)} %bitcast.12), channel_id=1, replica_groups=mesh['wa'=128,'y'=2,'c'=2] {'wa'}, dimensions={0} | all-to-all | bytes 786432 | tf_op jit(solution)/shard_map/all_to_all | solution.py:413
  105.5 0.9 spread.1
Async XLA Ops:
  1.7 8.5 %collective-permute-start.1 = (f32[384,128]{1,0:T(8,128)S(1)}, f32[384,128]{1,0:T(8,128)S(1)}, u32[]{:S(2)}, u32[]{:S(2)}) collective-permute-start(f32[384,128]{1,0:T(8,128)S(1)} %get-tuple-element.25), channel_id=1, source_target_pairs={{0,2},{2,0},{1,3},{3,1},{4,6},{6,4},{5,7},{7,5},{8,10},{10,8},{9,1... | collective-permute-start | bytes 589832 | tf_op jit(solution)/shard_map/ppermute | solution.py:417
  6.3 3.9 %collective-permute-start = (f32[384,128]{1,0:T(8,128)S(1)}, f32[384,128]{1,0:T(8,128)S(1)}, u32[]{:S(2)}, u32[]{:S(2)}) collective-permute-start(f32[384,128]{1,0:T(8,128)S(1)} %get-tuple-element.24.w_ref.w0_ref), channel_id=1, source_target_pairs={{0,1},{1,0},{2,3},{3,2},{4,5},{5,4},{6,7},{7,6},{8,9},{9,8},{10,11... | collective-permute-start | bytes 589832 | tf_op jit(solution)/shard_map/ppermute | solution.py:417
  10.2 3.3 %collective-permute-start.2 = (f32[384,128]{1,0:T(8,128)S(1)}, f32[384,128]{1,0:T(8,128)S(1)}, u32[]{:S(2)}, u32[]{:S(2)}) collective-permute-start(f32[384,128]{1,0:T(8,128)S(1)} %collective-permute-done.1.w_ref.w2_ref), channel_id=1, source_target_pairs={{0,1},{1,0},{2,3},{3,2},{4,5},{5,4},{6,7},{7,6},{8,9},{9,8},{10,11... | collective-permute-start | bytes 589832 | tf_op jit(solution)/shard_map/ppermute | solution.py:417
  14.0 25.8 %copy-start = (f32[6,128,128]{2,1,0:T(8,128)S(1)}, f32[6,128,128]{2,1,0:T(8,128)}, u32[]{:S(2)}) copy-start(f32[6,128,128]{2,1,0:T(8,128)} %inv_ref.1) | copy-start | bytes 1179652
  14.0 25.8 %copy-start.1 = (f32[5,128,128]{2,1,0:T(8,128)S(1)}, f32[5,128,128]{2,1,0:T(8,128)}, u32[]{:S(2)}) copy-start(f32[5,128,128]{2,1,0:T(8,128)} %mult_ref.1) | copy-start | bytes 983044
  16.3 51.8 %all-to-all-start = ((f32[256,1,384]{2,1,0:T(1,128)}), f32[256,1,384]{2,1,0:T(1,128)S(1)}, u32[]{:S(2)}, u32[]{:S(2)}) async-start(f32[256,1,384]{2,1,0:T(1,128)} %bitcast.5), calls=%async_computation | async-start | bytes 786432 | tf_op jit(solution)/shard_map/all_to_all | solution.py:413

commit v7 on v6

--- a/solution.py
+++ b/solution.py
@@ -323,14 +323,14 @@
     return rhs
 
 
-def matmul3(left, right, contract=((1,), (0,))):
-    left_h, left_l = split(left)
-    right_h, right_l = split(right)
-
-    def one(u, v):
-        return lax.dot_general(u, v, (contract, ((), ())), preferred_element_type=jnp.float32)
-
-    return one(left_h, right_h) + one(left_h, right_l) + one(left_l, right_h)
+def product_high(left, right, contract=((1,), (0,))):
+    return lax.dot_general(
+        left,
+        right,
+        (contract, ((), ())),
+        precision=lax.Precision.HIGHEST,
+        preferred_element_type=jnp.float32,
+    )
 
 
 def operator_kernel(inv_ref, mult_ref, high_ref, low_ref, g_ref, s_ref):
@@ -342,19 +342,19 @@
     for j in range(nblocks):
         rows = pl.ds(j * width, width)
         if j:
-            g_ref[rows, : j * width] = -matmul3(
+            g_ref[rows, : j * width] = -product_high(
                 mult_ref[j - 1], g_ref[pl.ds((j - 1) * width, width), : j * width]
             )
         g_ref[rows, j * width : (j + 1) * width] = eye
     for j in reversed(range(nblocks)):
         rows = pl.ds(j * width, width)
         own = (j + 1) * width
-        result = matmul3(inv_ref[j], g_ref[rows, :own])
+        result = product_high(inv_ref[j], g_ref[rows, :own])
         if j < nblocks - 1:
             result = jnp.concatenate(
                 [result, jnp.zeros((width, (nblocks - 1 - j) * width), jnp.float32)], axis=1
             )
-            result = result - matmul3(
+            result = result - product_high(
                 mult_ref[j], s_ref[pl.ds((j + 1) * width, width), :], ((0,), (0,))
             )
         s_ref[rows, :] = result

time: 107 us -> 107 us (level)
  Pallas kernels: 11.1 us -> 12.3 us
  waiting for transfers between devices: 27 us -> 25.8 us
    all_to_all x1, waiting for transfers between devices: 25 us -> 23.8 us  [exchange(): return lax.all_to_all(sent, axes, 0, 0, tiled=True).reshape(rows.shape)]
    pallas_call x10, Pallas kernels: 11.1 us -> 12.3 us  [call(): pl.pallas_call(kernel, out_shape=shapes, in_specs=specs, out_specs=[pl.Bl...]
  transfers between devices with their start and end apart: 4 -> 4, of which waited for: 3 -> 3; matrix products, arithmetic and copies ran while one was open for 0% -> 0% of each run, Pallas kernels for 5% -> 6%
where the time goes in v7:
time: 107 us; the launch traced here: 106 us
  blocking collectives  36.6 us (34%)
  starting transfers between devices  30.8 us (29%)
  waiting for transfers between devices  25.8 us (24%)
  Pallas kernels  12.3 us (11%)
    all_to_all x1, blocking collectives, exchange(): return lax.all_to_all(sent, axes, 0, 0, tiled=True).reshape(rows.shape)  36.6 us
    all_to_all x1, waiting for transfers between devices, exchange(): return lax.all_to_all(sent, axes, 0, 0, tiled=True).reshape(rows.shape)  23.8 us
    all_to_all x1, starting transfers between devices, exchange(): return lax.all_to_all(sent, axes, 0, 0, tiled=True).reshape(rows.shape)  23.5 us
    pallas_call x10, Pallas kernels, call(): pl.pallas_call(kernel, out_shape=shapes, in_specs=specs, out_specs=[pl.Bl...  12.3 us
    ppermute x3, starting transfers between devices, swap(): return lax.ppermute(value, axis, [(0, 1), (1, 0)])  7.32 us
  transfers between devices with their start and end apart: 4, of which 3 were waited for; matrix products, arithmetic and copies ran while one was open for 0% of the time, Pallas kernels for 6%

profile of v7, /device:TPU:6, one launch (start us, length us, event | category | flops | bytes accessed | tf_op | source)
XLA Modules:
  0.0 106.4 jit_solution(484111669263817919)
XLA Ops:
  0.6 1.0 send_half.1
  1.7 3.5 %collective-permute-start.1 = (f32[384,128]{1,0:T(8,128)S(1)}, f32[384,128]{1,0:T(8,128)S(1)}, u32[]{:S(2)}, u32[]{:S(2)}) collective-permute-start(f32[384,128]{1,0:T(8,128)S(1)} %get-tuple-element.25), channel_id=1, source_target_pairs={{0,2},{2,0},{1,3},{3,1},{4,6},{6,4},{5,7},{7,5},{8,10},{10,8},{9,1... | collective-permute-start | bytes 589832 | tf_op jit(solution)/shard_map/ppermute | solution.py:417
  5.2 1.1 %keep_half.1 = (f32[384,128]{1,0:T(8,128)S(1)}, bf16[96,192]{1,0:T(8,128)(2,1)S(1)}, bf16[128,192]{1,0:T(8,128)(2,1)S(1)}, f32[48,128]{1,0:T(8,128)S(1)}, f32[48...) custom-call(s32[1]{0:T(128)} %bitcast.y_ref, ...), custom_call_target="tpu_custom_call" | custom-call | bytes 1000000 | tf_op jit(solution)/shard_map/keep_half/pallas_call | solution.py:84
  6.3 1.9 %collective-permute-start = (f32[384,128]{1,0:T(8,128)S(1)}, f32[384,128]{1,0:T(8,128)S(1)}, u32[]{:S(2)}, u32[]{:S(2)}) collective-permute-start(f32[384,128]{1,0:T(8,128)S(1)} %get-tuple-element.24.w_ref.w0_ref), channel_id=1, source_target_pairs={{0,1},{1,0},{2,3},{3,2},{4,5},{5,4},{6,7},{7,6},{8,9},{9,8},{10,11... | collective-permute-start | bytes 589832 | tf_op jit(solution)/shard_map/ppermute | solution.py:417
  8.3 0.4 to_grid.4.g0
  8.7 1.5 %collective-permute-done.1.w_ref.w2_ref = f32[384,128]{1,0:T(8,128)S(1)} collective-permute-done((f32[384,128]{1,0:T(8,128)S(1)}, f32[384,128]{1,0:T(8,128)S(1)}, u32[]{:S(2)}, u32[]{:S(2)}) %collective-permute-start.1) | collective-permute-done | bytes 196640 | tf_op jit(solution)/shard_map/ppermute | solution.py:417
  10.2 0.0 collective-permute-done.w_ref
  10.2 1.9 %collective-permute-start.2 = (f32[384,128]{1,0:T(8,128)S(1)}, f32[384,128]{1,0:T(8,128)S(1)}, u32[]{:S(2)}, u32[]{:S(2)}) collective-permute-start(f32[384,128]{1,0:T(8,128)S(1)} %collective-permute-done.1.w_ref.w2_ref), channel_id=1, source_target_pairs={{0,1},{1,0},{2,3},{3,2},{4,5},{5,4},{6,7},{7,6},{8,9},{9,8},{10,11... | collective-permute-start | bytes 589832 | tf_op jit(solution)/shard_map/ppermute | solution.py:417
  12.2 0.4 to_grid.6.g2
  12.6 0.5 to_grid.5.g1
  13.1 0.5 collective-permute-done.2.w_ref
  13.6 0.4 to_grid.7.g3
  14.0 0.0 copy-start
  14.0 0.0 copy-start.1
  14.0 2.3 %to_rhs.1 = f32[768,128]{1,0:T(8,128)} custom-call(s32[1]{0:T(128)S(6)} %add.7.x_ref, f32[288,256]{1,0:T(8,128)S(1)} %to_grid.4.g0, f32[288,256]{1,0:T(8,128)S(1)} %to_grid.5.g1, f32[288,256]{1,0:T(8,128)S(1)} %to_grid.6.g2, f32[288,256]{1,0:T(8,128)S(1)} %to_grid.7.g3, f32[384,128]{1,0:T(8,128)S(1)} %get-tuple-element.24.w_ref.w0_ref, ...), custom_call_target="tpu_custom_call" | custom-call | flops 905969664 | bytes 1000000 | tf_op jit(solution)/shard_map/to_rhs/pallas_call | solution.py:84
  16.3 23.5 %all-to-all-start = ((f32[256,1,384]{2,1,0:T(1,128)}), f32[256,1,384]{2,1,0:T(1,128)S(1)}, u32[]{:S(2)}, u32[]{:S(2)}) async-start(f32[256,1,384]{2,1,0:T(1,128)} %bitcast.5), calls=%async_computation | async-start | bytes 786432 | tf_op jit(solution)/shard_map/all_to_all | solution.py:413
  39.8 0.0 copy-done
  39.8 0.0 copy-done.1
  39.8 4.4 %solve_operator.1 = (bf16[768,768]{1,0:T(8,128)(2,1)S(1)}, bf16[768,768]{1,0:T(8,128)(2,1)S(1)}) custom-call(f32[6,128,128]{2,1,0:T(8,128)S(1)} %copy-done, f32[5,128,128]{2,1,0:T(8,128)S(1)} %copy-done.1), custom_call_target="tpu_custom_call" | custom-call | flops 2768240640 | bytes 1000000 | tf_op jit(solution)/shard_map/solve_operator/pallas_call | solution.py:84
  44.2 23.8 %all-to-all-done = f32[256,1,384]{2,1,0:T(1,128)S(1)} async-done(((f32[256,1,384]{2,1,0:T(1,128)}), f32[256,1,384]{2,1,0:T(1,128)S(1)}, u32[]{:S(2)}, u32[]{:S(2)}) %all-to-all-start) | async-done | bytes 393248 | tf_op jit(solution)/shard_map/all_to_all | solution.py:413
  68.0 0.8 solve.1
  68.8 36.6 %all_to_all.10 = f32[128,1,768]{2,1,0:T(1,128)S(1)} all-to-all(f32[128,1,768]{2,1,0:T(1,128)S(1)} %bitcast.12), channel_id=1, replica_groups=mesh['wa'=128,'y'=2,'c'=2] {'wa'}, dimensions={0} | all-to-all | bytes 786432 | tf_op jit(solution)/shard_map/all_to_all | solution.py:413
  105.5 0.9 spread.1
Async XLA Ops:
  1.7 8.5 %collective-permute-start.1 = (f32[384,128]{1,0:T(8,128)S(1)}, f32[384,128]{1,0:T(8,128)S(1)}, u32[]{:S(2)}, u32[]{:S(2)}) collective-permute-start(f32[384,128]{1,0:T(8,128)S(1)} %get-tuple-element.25), channel_id=1, source_target_pairs={{0,2},{2,0},{1,3},{3,1},{4,6},{6,4},{5,7},{7,5},{8,10},{10,8},{9,1... | collective-permute-start | bytes 589832 | tf_op jit(solution)/shard_map/ppermute | solution.py:417
  6.3 3.9 %collective-permute-start = (f32[384,128]{1,0:T(8,128)S(1)}, f32[384,128]{1,0:T(8,128)S(1)}, u32[]{:S(2)}, u32[]{:S(2)}) collective-permute-start(f32[384,128]{1,0:T(8,128)S(1)} %get-tuple-element.24.w_ref.w0_ref), channel_id=1, source_target_pairs={{0,1},{1,0},{2,3},{3,2},{4,5},{5,4},{6,7},{7,6},{8,9},{9,8},{10,11... | collective-permute-start | bytes 589832 | tf_op jit(solution)/shard_map/ppermute | solution.py:417
  10.2 3.3 %collective-permute-start.2 = (f32[384,128]{1,0:T(8,128)S(1)}, f32[384,128]{1,0:T(8,128)S(1)}, u32[]{:S(2)}, u32[]{:S(2)}) collective-permute-start(f32[384,128]{1,0:T(8,128)S(1)} %collective-permute-done.1.w_ref.w2_ref), channel_id=1, source_target_pairs={{0,1},{1,0},{2,3},{3,2},{4,5},{5,4},{6,7},{7,6},{8,9},{9,8},{10,11... | collective-permute-start | bytes 589832 | tf_op jit(solution)/shard_map/ppermute | solution.py:417
  14.0 25.8 %copy-start = (f32[6,128,128]{2,1,0:T(8,128)S(1)}, f32[6,128,128]{2,1,0:T(8,128)}, u32[]{:S(2)}) copy-start(f32[6,128,128]{2,1,0:T(8,128)} %inv_ref.1) | copy-start | bytes 1179652
  14.0 25.8 %copy-start.1 = (f32[5,128,128]{2,1,0:T(8,128)S(1)}, f32[5,128,128]{2,1,0:T(8,128)}, u32[]{:S(2)}) copy-start(f32[5,128,128]{2,1,0:T(8,128)} %mult_ref.1) | copy-start | bytes 983044
  16.3 51.8 %all-to-all-start = ((f32[256,1,384]{2,1,0:T(1,128)}), f32[256,1,384]{2,1,0:T(1,128)S(1)}, u32[]{:S(2)}, u32[]{:S(2)}) async-start(f32[256,1,384]{2,1,0:T(1,128)} %bitcast.5), calls=%async_computation | async-start | bytes 786432 | tf_op jit(solution)/shard_map/all_to_all | solution.py:413

commit v8 on v7

--- a/solution.py
+++ b/solution.py
@@ -67,7 +67,7 @@
     modes_h, modes_l = split_np(to_modes)
     lanes_h, lanes_l = split_np(lanes)
     return dict(
-        to_grid=np.concatenate([grid_h, grid_h, grid_l], axis=1),
+        to_grid=np.block([[grid_h, grid_h], [grid_l, np.zeros_like(grid_l)]]),
         to_modes=np.block([[modes_h, modes_h], [modes_l, np.zeros_like(modes_l)]]),
         twist_re=twist_re,
         twist_im=twist_im,
@@ -180,7 +180,8 @@
     for row in range(HALF):
         modes = jnp.concatenate([load_modes(w_ref, 0, row), load_modes(w_ref, 1, row)], axis=1)
         high, low = split(modes)
-        sums = dot(table, jnp.concatenate([high, low, high], axis=0))
+        sums = dot(table, jnp.concatenate([high, low], axis=0))
+        sums = sums[: 2 * SLOT] + sums[2 * SLOT :]
         for field in range(2):
             lanes = slice(field * LANES, (field + 1) * LANES)
             re, im = sums[:SLOT, lanes], sums[SLOT:, lanes]

time: 107 us -> 107 us (level)
  transfers between devices with their start and end apart: 4 -> 4, of which waited for: 3 -> 3; matrix products, arithmetic and copies ran while one was open for 0% -> 0% of each run, Pallas kernels for 6% -> 7%
where the time goes in v8:
time: 107 us; the launch traced here: 106 us
  blocking collectives  36.6 us (34%)
  starting transfers between devices  30.8 us (29%)
  waiting for transfers between devices  25.8 us (24%)
  Pallas kernels  12.4 us (12%)
    all_to_all x1, blocking collectives, exchange(): return lax.all_to_all(sent, axes, 0, 0, tiled=True).reshape(rows.shape)  36.6 us
    all_to_all x1, waiting for transfers between devices, exchange(): return lax.all_to_all(sent, axes, 0, 0, tiled=True).reshape(rows.shape)  23.8 us
    all_to_all x1, starting transfers between devices, exchange(): return lax.all_to_all(sent, axes, 0, 0, tiled=True).reshape(rows.shape)  23.5 us
    pallas_call x10, Pallas kernels, call(): pl.pallas_call(kernel, out_shape=shapes, in_specs=specs, out_specs=[pl.Bl...  12.4 us
    ppermute x3, starting transfers between devices, swap(): return lax.ppermute(value, axis, [(0, 1), (1, 0)])  7.32 us
  transfers between devices with their start and end apart: 4, of which 3 were waited for; matrix products, arithmetic and copies ran while one was open for 0% of the time, Pallas kernels for 7%

profile of v8, /device:TPU:6, one launch (start us, length us, event | category | flops | bytes accessed | tf_op | source)
XLA Modules:
  0.0 106.4 jit_solution(12395195465672402207)
XLA Ops:
  0.6 1.0 send_half.1
  1.7 3.5 %collective-permute-start.1 = (f32[384,128]{1,0:T(8,128)S(1)}, f32[384,128]{1,0:T(8,128)S(1)}, u32[]{:S(2)}, u32[]{:S(2)}) collective-permute-start(f32[384,128]{1,0:T(8,128)S(1)} %get-tuple-element.25), channel_id=1, source_target_pairs={{0,2},{2,0},{1,3},{3,1},{4,6},{6,4},{5,7},{7,5},{8,10},{10,8},{9,1... | collective-permute-start | bytes 589832 | tf_op jit(solution)/shard_map/ppermute | solution.py:418
  5.2 1.1 %keep_half.1 = (f32[384,128]{1,0:T(8,128)S(1)}, bf16[192,128]{1,0:T(8,128)(2,1)S(1)}, bf16[128,192]{1,0:T(8,128)(2,1)S(1)}, f32[48,128]{1,0:T(8,128)S(1)}, f32[4...) custom-call(s32[1]{0:T(128)} %bitcast.y_ref, ...), custom_call_target="tpu_custom_call" | custom-call | bytes 1000000 | tf_op jit(solution)/shard_map/keep_half/pallas_call | solution.py:84
  6.3 1.9 %collective-permute-start = (f32[384,128]{1,0:T(8,128)S(1)}, f32[384,128]{1,0:T(8,128)S(1)}, u32[]{:S(2)}, u32[]{:S(2)}) collective-permute-start(f32[384,128]{1,0:T(8,128)S(1)} %get-tuple-element.24.w_ref.w0_ref), channel_id=1, source_target_pairs={{0,1},{1,0},{2,3},{3,2},{4,5},{5,4},{6,7},{7,6},{8,9},{9,8},{10,11... | collective-permute-start | bytes 589832 | tf_op jit(solution)/shard_map/ppermute | solution.py:418
  8.3 0.5 to_grid.4.g0
  8.7 1.5 %collective-permute-done.1.w_ref.w2_ref = f32[384,128]{1,0:T(8,128)S(1)} collective-permute-done((f32[384,128]{1,0:T(8,128)S(1)}, f32[384,128]{1,0:T(8,128)S(1)}, u32[]{:S(2)}, u32[]{:S(2)}) %collective-permute-start.1) | collective-permute-done | bytes 196640 | tf_op jit(solution)/shard_map/ppermute | solution.py:418
  10.2 0.0 collective-permute-done.w_ref
  10.2 1.9 %collective-permute-start.2 = (f32[384,128]{1,0:T(8,128)S(1)}, f32[384,128]{1,0:T(8,128)S(1)}, u32[]{:S(2)}, u32[]{:S(2)}) collective-permute-start(f32[384,128]{1,0:T(8,128)S(1)} %collective-permute-done.1.w_ref.w2_ref), channel_id=1, source_target_pairs={{0,1},{1,0},{2,3},{3,2},{4,5},{5,4},{6,7},{7,6},{8,9},{9,8},{10,11... | collective-permute-start | bytes 589832 | tf_op jit(solution)/shard_map/ppermute | solution.py:418
  12.2 0.5 to_grid.6.g2
  12.6 0.5 to_grid.5.g1
  13.1 0.4 collective-permute-done.2.w_ref
  13.6 0.5 to_grid.7.g3
  14.0 0.0 copy-start
  14.0 0.0 copy-start.1
  14.0 2.3 %to_rhs.1 = f32[768,128]{1,0:T(8,128)} custom-call(s32[1]{0:T(128)S(6)} %add.7.x_ref, f32[288,256]{1,0:T(8,128)S(1)} %to_grid.4.g0, f32[288,256]{1,0:T(8,128)S(1)} %to_grid.5.g1, f32[288,256]{1,0:T(8,128)S(1)} %to_grid.6.g2, f32[288,256]{1,0:T(8,128)S(1)} %to_grid.7.g3, f32[384,128]{1,0:T(8,128)S(1)} %get-tuple-element.24.w_ref.w0_ref, ...), custom_call_target="tpu_custom_call" | custom-call | flops 905969664 | bytes 1000000 | tf_op jit(solution)/shard_map/to_rhs/pallas_call | solution.py:84
  16.3 23.5 %all-to-all-start = ((f32[256,1,384]{2,1,0:T(1,128)}), f32[256,1,384]{2,1,0:T(1,128)S(1)}, u32[]{:S(2)}, u32[]{:S(2)}) async-start(f32[256,1,384]{2,1,0:T(1,128)} %bitcast.5), calls=%async_computation | async-start | bytes 786432 | tf_op jit(solution)/shard_map/all_to_all | solution.py:414
  39.8 0.0 copy-done
  39.8 0.0 copy-done.1
  39.9 4.4 %solve_operator.1 = (bf16[768,768]{1,0:T(8,128)(2,1)S(1)}, bf16[768,768]{1,0:T(8,128)(2,1)S(1)}) custom-call(f32[6,128,128]{2,1,0:T(8,128)S(1)} %copy-done, f32[5,128,128]{2,1,0:T(8,128)S(1)} %copy-done.1), custom_call_target="tpu_custom_call" | custom-call | flops 2768240640 | bytes 1000000 | tf_op jit(solution)/shard_map/solve_operator/pallas_call | solution.py:84
  44.2 23.8 %all-to-all-done = f32[256,1,384]{2,1,0:T(1,128)S(1)} async-done(((f32[256,1,384]{2,1,0:T(1,128)}), f32[256,1,384]{2,1,0:T(1,128)S(1)}, u32[]{:S(2)}, u32[]{:S(2)}) %all-to-all-start) | async-done | bytes 393248 | tf_op jit(solution)/shard_map/all_to_all | solution.py:414
  68.1 0.8 solve.1
  68.9 36.6 %all_to_all.10 = f32[128,1,768]{2,1,0:T(1,128)S(1)} all-to-all(f32[128,1,768]{2,1,0:T(1,128)S(1)} %bitcast.12), channel_id=1, replica_groups=mesh['wa'=128,'y'=2,'c'=2] {'wa'}, dimensions={0} | all-to-all | bytes 786432 | tf_op jit(solution)/shard_map/all_to_all | solution.py:414
  105.5 0.9 spread.1
Async XLA Ops:
  1.7 8.5 %collective-permute-start.1 = (f32[384,128]{1,0:T(8,128)S(1)}, f32[384,128]{1,0:T(8,128)S(1)}, u32[]{:S(2)}, u32[]{:S(2)}) collective-permute-start(f32[384,128]{1,0:T(8,128)S(1)} %get-tuple-element.25), channel_id=1, source_target_pairs={{0,2},{2,0},{1,3},{3,1},{4,6},{6,4},{5,7},{7,5},{8,10},{10,8},{9,1... | collective-permute-start | bytes 589832 | tf_op jit(solution)/shard_map/ppermute | solution.py:418
  6.3 3.9 %collective-permute-start = (f32[384,128]{1,0:T(8,128)S(1)}, f32[384,128]{1,0:T(8,128)S(1)}, u32[]{:S(2)}, u32[]{:S(2)}) collective-permute-start(f32[384,128]{1,0:T(8,128)S(1)} %get-tuple-element.24.w_ref.w0_ref), channel_id=1, source_target_pairs={{0,1},{1,0},{2,3},{3,2},{4,5},{5,4},{6,7},{7,6},{8,9},{9,8},{10,11... | collective-permute-start | bytes 589832 | tf_op jit(solution)/shard_map/ppermute | solution.py:418
  10.2 3.3 %collective-permute-start.2 = (f32[384,128]{1,0:T(8,128)S(1)}, f32[384,128]{1,0:T(8,128)S(1)}, u32[]{:S(2)}, u32[]{:S(2)}) collective-permute-start(f32[384,128]{1,0:T(8,128)S(1)} %collective-permute-done.1.w_ref.w2_ref), channel_id=1, source_target_pairs={{0,1},{1,0},{2,3},{3,2},{4,5},{5,4},{6,7},{7,6},{8,9},{9,8},{10,11... | collective-permute-start | bytes 589832 | tf_op jit(solution)/shard_map/ppermute | solution.py:418
  14.0 25.8 %copy-start = (f32[6,128,128]{2,1,0:T(8,128)S(1)}, f32[6,128,128]{2,1,0:T(8,128)}, u32[]{:S(2)}) copy-start(f32[6,128,128]{2,1,0:T(8,128)} %inv_ref.1) | copy-start | bytes 1179652
  14.0 25.8 %copy-start.1 = (f32[5,128,128]{2,1,0:T(8,128)S(1)}, f32[5,128,128]{2,1,0:T(8,128)}, u32[]{:S(2)}) copy-start(f32[5,128,128]{2,1,0:T(8,128)} %mult_ref.1) | copy-start | bytes 983044
  16.3 51.8 %all-to-all-start = ((f32[256,1,384]{2,1,0:T(1,128)}), f32[256,1,384]{2,1,0:T(1,128)S(1)}, u32[]{:S(2)}, u32[]{:S(2)}) async-start(f32[256,1,384]{2,1,0:T(1,128)} %bitcast.5), calls=%async_computation | async-start | bytes 786432 | tf_op jit(solution)/shard_map/all_to_all | solution.py:414
